TPU v7x, 256 devices: a whole 4x4x8 slice. The times are simulated.
256 devices in a mesh: dp: 16 (over x_lo, z), tensor: 16 (over x_hi, y, core).
Axes of the slice: x: 4 (x_hi: 2, x_lo: 2; x = x_hi * 2 + x_lo), y: 4, z: 8, core: 2. Of those that a mesh axis runs over, the one named last changes fastest.
Arguments:
- hidden: bfloat16 [4096, 8192], P('dp', 'tensor'), may hold values from -6 to 6
- connector: bfloat16 [8192, 3584], P('tensor'), may hold values from -0.0625 to 0.0625
- routing: int32 [4096, 1], P('dp'), may hold values from 0 to 15; in each aligned block of 256 rows (0 to 255, 256 to 511, ...) at most 32 rows name the same one
- talker_in: bfloat16 [8192, 3584], P(('dp', 'tensor')), may hold values from -6 to 6
- norm_gain: float32 [3584], replicated, may hold values from 0.25 to 1.75
- kv_weight: bfloat16 [3584, 1024], replicated, may hold values from -0.09375 to 0.09375
- kv_grad: bfloat16 [8192, 1024], P(('dp', 'tensor')), may hold values from -24 to 24
Outputs:
- hidden_grad: bfloat16 [4096, 8192], P('dp', 'tensor')
- connector_grad: float32 [8192, 3584], P('tensor', 'dp')
- kv_weight_grad: float32 [3584, 1024], P(None, ('dp', 'tensor'))
Inputs may be any that keep to these rules, and one draw needn't show every extreme that they name: `routing`: among the 256 rows of one index of dp, at most 32 go to one shard.
All inputs are finite; a program needn't handle non-finite values.
Results may differ from a plain program's by a relative error of at most 0.005.
Values may be sent and summed in bfloat16 or wider, within the bound.
A program may use at most 64 MiB of HBM per device.

v0:
```python
import math

import jax
import jax.numpy as jnp
from jax import lax
from jax.sharding import Mesh
from jax.sharding import PartitionSpec as P

TENSOR = ("tensor_0", "tensor_1", "tensor_2")
DP_TENSOR = ("dp", "tensor_0", "tensor_1", "tensor_2")


CONTRACT_LAST = (((1,), (1,)), ((), ()))
CONTRACT_FIRST = (((0,), (0,)), ((), ()))


def cut_along(value, dim, size):
    before, after = (value.shape[:dim], value.shape[dim + 1 :])
    return jnp.moveaxis(value.reshape(*before, size, -1, *after), dim, 0)


def sum_at_owner(value, axis, dim):
    size = lax.axis_size(axis)
    pieces = lax.all_to_all(cut_along(value, dim, size), axis, 0, 0, tiled=True)
    return jnp.sum(pieces, axis=0)


def sent_to_all(value, axis):
    copies = jnp.broadcast_to(value, (lax.axis_size(axis), *value.shape))
    return lax.all_to_all(copies, axis, split_axis=0, concat_axis=0, tiled=True)


def in_order(pieces, dim):
    dims = list(pieces.shape[1:])
    dims[dim] *= pieces.shape[0]
    return jnp.moveaxis(pieces, 0, dim).reshape(dims)


def gather_axes(value, axes, dim):
    far, near = axes
    pieces = sent_to_all(sent_to_all(value, far), near)
    return in_order(pieces.swapaxes(0, 1).reshape(-1, *value.shape), dim)


def on_device(hidden, connector, routing, talker_in, norm_gain, kv_weight, kv_grad):
    dp_count = lax.axis_size("dp")
    tensor_count = lax.axis_size(TENSOR)
    rows_dev = hidden.shape[0]
    capacity = talker_in.shape[0]
    factor = 1.0 / math.sqrt(rows_dev * dp_count)
    route_rows = routing[:, 0]
    shards = jnp.arange(tensor_count, dtype=jnp.int32)
    onehot = (route_rows[:, None] == shards[None, :]).astype(jnp.int32)
    ranks = jnp.sum((jnp.cumsum(onehot, axis=0) - 1) * onehot, axis=1)
    slot_ids = route_rows * capacity + ranks
    counts = jnp.sum(onehot, axis=0)
    tensor_pos = lax.axis_index(TENSOR)
    own_count = jnp.sum(jnp.where(shards == tensor_pos, counts, 0))
    usable = jnp.arange(capacity, dtype=jnp.int32) < own_count
    masked = jnp.where(usable[:, None], kv_grad, jnp.zeros_like(kv_grad))
    inputs = talker_in.astype(jnp.float32)
    inv_rms = lax.rsqrt(jnp.mean(inputs * inputs, axis=1, keepdims=True) + 1e-06)
    scaled = inputs * inv_rms
    normed = (scaled * norm_gain).astype(jnp.bfloat16)
    back_grad = lax.dot_general(
        masked, kv_weight, CONTRACT_LAST, preferred_element_type=jnp.float32
    )
    gain_back = norm_gain * back_grad
    talker_grad = (
        inv_rms * (gain_back - scaled * jnp.mean(gain_back * scaled, axis=1, keepdims=True))
    ).astype(jnp.bfloat16)
    col_count = masked.shape[1]
    per_dev = col_count // (dp_count * tensor_count)
    group_rows = lax.all_gather(normed, TENSOR, axis=0, tiled=True)
    regrouped = masked.reshape(capacity, dp_count, tensor_count, per_dev)
    regrouped = regrouped.transpose(0, 2, 1, 3).reshape(capacity, col_count)
    group_cols = lax.all_to_all(regrouped, TENSOR, split_axis=1, concat_axis=0, tiled=True)
    block_terms = (
        lax.dot_general(group_rows, group_cols, CONTRACT_FIRST, preferred_element_type=jnp.float32)
        * factor
    )
    kv_weight_grad = sum_at_owner(block_terms, "dp", 1)
    gathered = gather_axes(talker_grad, (("tensor_0", "tensor_1"), "tensor_2"), 0)
    row_grad = jnp.take(gathered, slot_ids, axis=0)
    hidden_grad = lax.dot_general(
        row_grad, connector, CONTRACT_LAST, preferred_element_type=jnp.float32
    ).astype(jnp.bfloat16)
    conn_terms = (
        lax.dot_general(hidden, row_grad, CONTRACT_FIRST, preferred_element_type=jnp.float32)
        * factor
    )
    connector_grad = lax.psum_scatter(conn_terms, "dp", scatter_dimension=1, tiled=True)
    return (hidden_grad, connector_grad, kv_weight_grad)


def solution(mesh):
    finer = Mesh(
        mesh.devices.reshape(mesh.shape["dp"], 2, 4, 2), ("dp", "tensor_0", "tensor_1", "tensor_2")
    )
    return jax.shard_map(
        on_device,
        mesh=finer,
        in_specs=(
            P("dp", TENSOR),
            P(TENSOR, None),
            P("dp", None),
            P(DP_TENSOR, None),
            P(),
            P(),
            P(DP_TENSOR, None),
        ),
        out_specs=(P("dp", TENSOR), P(TENSOR, "dp"), P(None, DP_TENSOR)),
        check_vma=False,
    )
```

profile of v0, /device:TPU:8, one launch (start us, length us, event | category | flops | bytes accessed | tf_op | source)
XLA Modules:
  0.0 196.0 jit_solution(6129102235819686993)
XLA Ops:
  8.0 0.0 copy-start
  8.0 0.0 all-gather.2.cloned.1.call-start
  8.1 1.1 fusion.8
  9.2 0.7 fusion.11
  9.9 0.6 reduce-window.6
  10.5 0.2 slice_reduce_fusion
  10.7 0.9 fusion.10
  11.6 0.6 fusion.12
  12.2 0.6 iota_compare_fusion.2
  12.9 1.0 copy.15
  13.9 0.0 copy-start.1
  13.9 0.0 copy-start.2
  13.9 5.6 %fusion.3 = (f32[32]{0:T(128)S(1)}, f32[32,3584]{1,0:T(8,128)S(1)}) fusion(bf16[32,3584]{1,0:T(8,128)(2,1)} %param.10, f32[32]{0:T(128)S(1)} %add_rsqrt_fusion, bf16[32,1024]{0,1:T(8,128)(2,1)S(1)} %broadcast_select_fusion.3, bf16[3584,1024]{1,0:T(8,128)(2,1)} %param.12, f32[3584]{0:T(1024)} %param.11), kind=kOutput, calls=%fused_computation.11 | convolution fusion | flops 235454432 | bytes 8108288 | tf_op jit(solution)/shard_map/dot_general | solution.py:65
  19.5 0.0 copy-start.3
  19.6 0.0 copy-done.1
  19.6 0.0 copy-done.2
  19.6 0.9 fusion.7
  20.4 0.0 all-gather.2.cloned.1.call-update
  20.5 1.4 broadcast_in_dim.41
  21.9 7.4 %all-to-all-start = ((bf16[8,32,3584]{2,1,0:T(8,128)(2,1)}), bf16[8,32,3584]{2,1,0:T(8,128)(2,1)S(1)}, u32[]{:S(2)}, u32[]{:S(2)}) async-start(bf16[8,32,3584]{2,1,0:T(8,128)(2,1)} %broadcast_in_dim.41), calls=%async_computation | async-start | bytes 3670016 | tf_op jit(solution)/shard_map/all_to_all | solution.py:30
  29.2 0.0 reduce-scatter.2.cloned.1.call-start
  29.2 0.0 copy-done.3
  29.3 25.4 %all-to-all-done = bf16[8,32,3584]{2,1,0:T(8,128)(2,1)S(1)} async-done(((bf16[8,32,3584]{2,1,0:T(8,128)(2,1)}), bf16[8,32,3584]{2,1,0:T(8,128)(2,1)S(1)}, u32[]{:S(2)}, u32[]{:S(2)}) %all-to-all-start) | async-done | bytes 1835040 | tf_op jit(solution)/shard_map/all_to_all | solution.py:30
  54.7 0.4 broadcast_in_dim.42
  55.1 6.7 %all_to_all.34 = bf16[2,8,32,3584]{3,2,1,0:T(8,128)(2,1)S(1)} all-to-all(bf16[2,8,32,3584]{3,2,1,0:T(8,128)(2,1)S(1)} %broadcast_in_dim.42), channel_id=1, replica_groups=mesh['dp'=16,'tensor_0'=2,'tensor_1'=4,'tensor_2'=2] {'tensor_2'}, dimensions={0} | all-to-all | bytes 7340032 | tf_op jit(solution)/shard_map/all_to_all | solution.py:30
  61.7 2.0 %copy.16 = bf16[8,2,32,3584]{3,2,1,0:T(8,128)(2,1)} copy(bf16[8,2,32,3584]{3,2,0,1:T(8,128)(2,1)S(1)} %bitcast.42) | data formatting | bytes 7340032 | tf_op jit(solution)/shard_map/transpose | solution.py:42
  63.8 6.0 %gather_fusion = bf16[256,3584]{1,0:T(8,128)(2,1)S(1)} fusion(bf16[512,3584]{1,0:T(8,128)(2,1)} %bitcast.41, s32[1024]{0:T(1024)S(1)} %pad_clamp_fusion), kind=kCustom, calls=%fused_computation | custom fusion | bytes 3671040 | tf_op jit(solution)/shard_map/jit(_take)/gather | solution.py:84
  69.8 0.0 copy-done
  69.8 4.2 %multiply_bitcast_fusion = f32[512,3584]{0,1:T(8,128)} fusion(bf16[256,512]{1,0:T(8,128)(2,1)S(1)} %copy-done, bf16[256,3584]{1,0:T(8,128)(2,1)S(1)} %gather_fusion, pred[256]{0:T(512)(128)(4,1)S(1)} %get-tuple-element.5), kind=kOutput, calls=%fused_computation.1 | convolution fusion | flops 942276608 | bytes 9437440 | tf_op jit(solution)/shard_map/dot_general | solution.py:89
  74.1 0.0 reduce-scatter.2.cloned.1.call-update
  74.1 0.3 copy.18
  74.4 0.1 reshape.71
  74.5 12.2 %all_to_all.35 = bf16[16,2,1024]{2,1,0:T(2,128)(2,1)S(1)} all-to-all(bf16[16,2,1024]{2,1,0:T(2,128)(2,1)S(1)} %reshape.71), channel_id=1, replica_groups=mesh['dp'=16,'tensor_0'=2,'tensor_1'=4,'tensor_2'=2] {'tensor_0','tensor..., dimensions={0} | all-to-all | bytes 131072 | tf_op jit(solution)/shard_map/all_to_all | solution.py:77
  86.7 0.1 reshape.72
  86.9 4.4 %all-gather.2.cloned.1.call-done = bf16[512,3584]{1,0:T(8,128)(2,1)} async-done(((bf16[32,3584]{1,0:T(8,128)(2,1)}), bf16[512,3584]{1,0:T(8,128)(2,1)}) %all-gather.2.cloned.1.call-update) | async-done | bytes 3670032 | tf_op jit(solution)/shard_map/all_gather | solution.py:74
  91.3 2.8 %convolution_multiply_fusion = f32[3584,64]{0,1:T(8,128)S(1)} fusion(bf16[512,3584]{1,0:T(8,128)(2,1)} %all-gather.2.cloned.1.call-done, bf16[512,64]{1,0:T(8,128)(2,1)S(1)} %bitcast.46), kind=kOutput, calls=%fused_computation.2 | convolution fusion | flops 235110400 | bytes 4653056 | tf_op jit(solution)/shard_map/dot_general | solution.py:79
  94.1 1.2 reshape.60
  95.3 7.2 %all-to-all-start.3 = ((f32[16,3584,4]{1,2,0:T(4,128)}), f32[16,3584,4]{1,2,0:T(4,128)S(1)}, u32[]{:S(2)}, u32[]{:S(2)}) async-start(f32[16,3584,4]{1,2,0:T(4,128)} %bitcast.43), calls=%async_computation.4 | async-start | bytes 1835008 | tf_op jit(solution)/shard_map/all_to_all | solution.py:24
  102.5 3.9 %convolution_convert_fusion = bf16[256,512]{1,0:T(8,128)(2,1)} fusion(bf16[512,3584]{1,0:T(8,128)(2,1)} %param.8, bf16[256,3584]{1,0:T(8,128)(2,1)S(1)} %gather_fusion, pred[256]{0:T(512)(128)(4,1)S(1)} %get-tuple-element.5), kind=kOutput, calls=%fused_computation.5 | convolution fusion | flops 940572672 | bytes 5767424 | tf_op jit(solution)/shard_map/dot_general | solution.py:85
  106.5 32.0 %all-to-all-done.3 = f32[16,3584,4]{1,2,0:T(4,128)S(1)} async-done(((f32[16,3584,4]{1,2,0:T(4,128)}), f32[16,3584,4]{1,2,0:T(4,128)S(1)}, u32[]{:S(2)}, u32[]{:S(2)}) %all-to-all-start.3) | async-done | bytes 917536 | tf_op jit(solution)/shard_map/all_to_all | solution.py:24
  138.4 0.8 reduce_sum.62
  139.2 49.3 %reduce-scatter.2.cloned.1.call-done = f32[512,224]{0,1:T(8,128)} async-done(((f32[512,3584]{0,1:T(8,128)}), f32[512,224]{0,1:T(8,128)}) %reduce-scatter.2.cloned.1.call-update) | async-done | bytes 458768 | tf_op jit(solution)/shard_map/reduce_scatter | solution.py:92
  (8 shorter events, 0.2 us)
Async XLA Ops:
  8.0 61.8 %copy-start = (bf16[256,512]{1,0:T(8,128)(2,1)S(1)}, bf16[256,512]{1,0:T(8,128)(2,1)}, u32[]{:S(2)}) copy-start(bf16[256,512]{1,0:T(8,128)(2,1)} %param.7) | copy-start | bytes 786436
  8.0 83.2 %all-gather.2.cloned.1.call-start = ((), (), s32[]{:S(2)}) async-start(), calls=%async_computation.6 | async-start | bytes 3899392 | tf_op jit(solution)/shard_map/all_gather | solution.py:74
  13.9 5.6 %copy-start.1 = (bf16[32,3584]{1,0:T(8,128)(2,1)S(1)}, bf16[32,3584]{1,0:T(8,128)(2,1)}, u32[]{:S(2)}) copy-start(bf16[32,3584]{1,0:T(8,128)(2,1)} %param.10) | copy-start | bytes 688132
  13.9 5.6 %copy-start.2 = (f32[3584]{0:T(1024)S(1)}, f32[3584]{0:T(1024)}, u32[]{:S(2)}) copy-start(f32[3584]{0:T(1024)} %param.11) | copy-start | bytes 43012
  19.5 9.7 %copy-start.3 = (s32[256,1]{0,1:T(1,128)S(1)}, s32[256,1]{0,1:T(1,128)}, u32[]{:S(2)}) copy-start(s32[256,1]{0,1:T(1,128)} %param.9) | copy-start | bytes 3076
  21.9 32.8 %all-to-all-start = ((bf16[8,32,3584]{2,1,0:T(8,128)(2,1)}), bf16[8,32,3584]{2,1,0:T(8,128)(2,1)S(1)}, u32[]{:S(2)}, u32[]{:S(2)}) async-start(bf16[8,32,3584]{2,1,0:T(8,128)(2,1)} %broadcast_in_dim.41), calls=%async_computation | async-start | bytes 3670016 | tf_op jit(solution)/shard_map/all_to_all | solution.py:30
  29.2 159.3 %reduce-scatter.2.cloned.1.call-start = ((), (), s32[]{:S(2)}) async-start(), calls=%async_computation.5 | async-start | bytes 7798784 | tf_op jit(solution)/shard_map/reduce_scatter | solution.py:92
  95.3 43.1 %all-to-all-start.3 = ((f32[16,3584,4]{1,2,0:T(4,128)}), f32[16,3584,4]{1,2,0:T(4,128)S(1)}, u32[]{:S(2)}, u32[]{:S(2)}) async-start(f32[16,3584,4]{1,2,0:T(4,128)} %bitcast.43), calls=%async_computation.4 | async-start | bytes 1835008 | tf_op jit(solution)/shard_map/all_to_all | solution.py:24
Sparse Core Ops, SparseCore 0:
  20.6 70.6 all-gather.1
Sparse Core Ops, SparseCore 1:
  74.2 114.3 reduce-scatter.1
where the time goes:
time: 196 us
  waiting for transfers between devices  111 us (57%)
  blocking collectives  18.9 us (10%)
  matrix products  16.6 us (8%)
  between operations  15.6 us (8%)
  starting transfers between devices  14.7 us (8%)
  local copies, waits for them, and re-layouts  12.8 us (7%)
  other arithmetic  6.28 us (3%)
    reduce_scatter x1, waiting for transfers between devices, on_device(): lax.psum_scatter(conn_terms, 'dp', scatter_dimension=1, tiled=True)  49.3 us
    all_to_all x1, waiting for transfers between devices, sum_at_owner(): pieces = lax.all_to_all(cut_along(value, dim, size), axis, 0, 0, tiled=True)  32 us
    all_to_all x1, waiting for transfers between devices, sent_to_all(): return lax.all_to_all(copies, axis, split_axis=0, concat_axis=0, tiled=True)  25.4 us
    all_to_all x1, blocking collectives, on_device(): lax.all_to_all(regrouped, TENSOR, split_axis=1, concat_axis=0, tiled=True)  12.2 us
    all_to_all x1, starting transfers between devices, sent_to_all(): return lax.all_to_all(copies, axis, split_axis=0, concat_axis=0, tiled=True)  7.38 us
    all_to_all x1, starting transfers between devices, sum_at_owner(): pieces = lax.all_to_all(cut_along(value, dim, size), axis, 0, 0, tiled=True)  7.24 us
    all_to_all x1, blocking collectives, sent_to_all(): return lax.all_to_all(copies, axis, split_axis=0, concat_axis=0, tiled=True)  6.68 us
    gather x1, local copies, waits for them, and re-layouts, on_device(): row_grad = jnp.take(gathered, slot_ids, axis=0)  6.04 us
  transfers between devices with their start and end apart: 4, of which 4 were waited for; matrix products, arithmetic and copies ran while one was open for 12% of the time, Pallas kernels for 0%

commit v1 on v0

v1 whole, which is shorter than its diff:
```python
import math

import jax
import jax.numpy as jnp
from jax import lax
from jax.experimental import pallas as pl
from jax.experimental.pallas import tpu as pltpu
from jax.sharding import PartitionSpec as P

MESH = pl.DeviceIdType.MESH
CONTRACT_LAST = (((1,), (1,)), ((), ()))
CONTRACT_FIRST = (((0,), (0,)), ((), ()))

NZ = 8
NY = 4


class Place:
    def __init__(self):
        self.dp = lax.axis_index("dp")
        self.t = lax.axis_index("tensor")
        self.z = lax.rem(self.dp, NZ)
        self.xl = lax.div(self.dp, NZ)
        self.core = lax.rem(self.t, 2)
        self.y = lax.rem(lax.div(self.t, 2), NY)
        self.xh = lax.div(self.t, 2 * NY)

    def tensor(self, xh, y, core):
        return xh * (2 * NY) + lax.rem(y + NY, NY) * 2 + core

    def at_y(self, step):
        return (self.dp, self.tensor(self.xh, self.y + step, self.core))

    def at_z(self, step):
        return (self.xl * NZ + lax.rem(self.z + step + NZ, NZ), self.t)

    def across(self):
        return (self.dp, self.tensor(1 - self.xh, self.y, self.core))

    def sibling(self):
        return (self.dp, self.tensor(self.xh, self.y, 1 - self.core))


def greet(devices):
    barrier = pltpu.get_barrier_semaphore()
    for device in devices:
        pl.semaphore_signal(barrier, inc=1, device_id=device, device_id_type=MESH)
    pl.semaphore_wait(barrier, len(devices))


class Sends:
    def __init__(self, send_sems, recv_sems):
        self.send_sems, self.recv_sems = send_sems, recv_sems
        self.open = []

    def send(self, src, dst, key, device):
        copy = pltpu.make_async_remote_copy(
            src_ref=src,
            dst_ref=dst,
            send_sem=self.send_sems.at[key],
            recv_sem=self.recv_sems.at[key],
            device_id=device,
            device_id_type=MESH,
        )
        copy.start()
        self.open.append(copy)

    def arrived(self, dst, key, device):
        pltpu.make_async_remote_copy(
            src_ref=dst,
            dst_ref=dst,
            send_sem=self.send_sems.at[key],
            recv_sem=self.recv_sems.at[key],
            device_id=device,
            device_id_type=MESH,
        ).wait_recv()

    def drain(self):
        for copy in self.open:
            copy.wait_send()


GROUP_KEYS = 12 + 2 + 16


def key_y(direction, far, kind):
    return direction * 6 + far * 3 + kind


def key_x(half):
    return 12 + half


def key_s(hop, half):
    return 14 + hop * 2 + half


class GroupGather:
    def __init__(self, place, own, slot, sends, base):
        self.place, self.own, self.slot = place, own, slot
        self.sends, self.base = sends, base

    def block(self, far, step):
        p = self.place
        return p.tensor(1 - p.xh if far else p.xh, p.y + step, p.core)

    def twin(self, far, step):
        p = self.place
        return p.tensor(1 - p.xh if far else p.xh, p.y + step, 1 - p.core)

    def hop(self, far, step):
        return far * 4 + step % 4

    def share(self, src, far, step, half):
        self.sends.send(
            src,
            self.slot(self.block(far, step), half),
            self.base + key_s(self.hop(far, step), half),
            self.place.sibling(),
        )

    def to_y(self, src, far, half, direction):
        step = 1 if direction == 0 else -1
        self.sends.send(
            src,
            self.slot(self.block(far, 0), half),
            self.base + key_y(direction, far, half),
            self.place.at_y(step),
        )

    def start(self):
        for half in (0, 1):
            self.to_y(self.own(half), 0, half, 0)
            self.to_y(self.own(1 - half), 0, 1 - half, 1)
            self.sends.send(
                self.own(half),
                self.slot(self.block(0, 0), half),
                self.base + key_x(half),
                self.place.across(),
            )
        for half in (0, 1):
            self.share(self.own(half), 0, 0, half)

    def take_x(self, half):
        dst = self.slot(self.block(1, 0), half)
        self.sends.arrived(dst, self.base + key_x(half), self.place.across())
        self.to_y(dst, 1, half, 0)
        self.to_y(dst, 1, half, 1)
        self.share(dst, 1, 0, half)

    def take_y(self, far, half, direction):
        step = -1 if direction == 0 else 1
        dst = self.slot(self.block(far, step), half)
        self.sends.arrived(
            dst, self.base + key_y(direction, far, half), self.place.at_y(step)
        )
        if half == direction:
            self.sends.send(
                dst,
                dst,
                self.base + key_y(direction, far, 2),
                self.place.at_y(-step),
            )
        self.share(dst, far, step, half)

    def take_far(self, far, direction):
        step = -1 if direction == 0 else 1
        half = direction
        dst = self.slot(self.block(far, 2 * step), half)
        self.sends.arrived(
            dst, self.base + key_y(direction, far, 2), self.place.at_y(step)
        )
        self.share(dst, far, 2, half)

    def take_shared(self):
        for far in (0, 1):
            for step in (0, 1, 2, 3):
                for half in (0, 1):
                    self.sends.arrived(
                        self.slot(self.twin(far, step), half),
                        self.base + key_s(self.hop(far, step), half),
                        self.place.sibling(),
                    )


def gather_inputs(talker_ref, kv_ref, hidden_ref, talkers, kvs, hiddens, send_sems, recv_sems, own_sems):
    place = Place()
    greet(
        [place.at_y(1), place.at_y(-1), place.across(), place.sibling(), place.at_z(1), place.at_z(-1)]
    )
    sends = Sends(send_sems, recv_sems)
    half_rows = talker_ref.shape[0] // 2
    half_hidden = hidden_ref.shape[0] // 2
    kept = [
        pltpu.make_async_copy(talker_ref, talkers.at[place.t], own_sems.at[0]),
        pltpu.make_async_copy(kv_ref, kvs.at[place.t], own_sems.at[1]),
        pltpu.make_async_copy(hidden_ref, hiddens.at[place.z], own_sems.at[2]),
    ]

    def gather(own_ref, slots, base):
        return GroupGather(
            place,
            lambda half: own_ref.at[pl.ds(half * half_rows, half_rows)],
            lambda block, half: slots.at[block, pl.ds(half * half_rows, half_rows)],
            sends,
            base,
        )

    pair = (gather(talker_ref, talkers, 0), gather(kv_ref, kvs, GROUP_KEYS))
    z_base = 2 * GROUP_KEYS

    def z_slot(step, part=None):
        slot = hiddens.at[lax.rem(place.z + step + NZ, NZ)]
        if part is None:
            return slot
        return slot.at[pl.ds(part * half_hidden, half_hidden)]

    def pass_z(hop):
        for direction, step in ((0, -1), (1, 1)):
            if hop:
                sends.arrived(z_slot(hop * step), z_base + direction * 4 + hop - 1, place.at_z(step))
            part = direction if hop == 3 else None
            if hop:
                src = z_slot(hop * step, part)
            else:
                src = hidden_ref
            sends.send(
                src, z_slot(hop * step, part), z_base + direction * 4 + hop, place.at_z(-step)
            )

    pass_z(0)
    for g in pair:
        g.start()
    for copy in kept:
        copy.start()
    for direction in (0, 1):
        for g in pair:
            g.take_y(0, direction, direction)
    for g in pair:
        g.take_x(0)
    pass_z(1)
    for direction in (0, 1):
        for g in pair:
            g.take_y(0, 1 - direction, direction)
    for g in pair:
        g.take_x(1)
    for direction in (0, 1):
        for g in pair:
            g.take_far(0, direction)
    pass_z(2)
    for half in (0, 1):
        for direction in (0, 1):
            for g in pair:
                g.take_y(1, half, direction)
    pass_z(3)
    for direction in (0, 1):
        for g in pair:
            g.take_far(1, direction)
    for g in pair:
        g.take_shared()
    for direction, step in ((0, -1), (1, 1)):
        sends.arrived(z_slot(4 * step, direction), z_base + direction * 4 + 3, place.at_z(step))
    for copy in kept:
        copy.wait()
    sends.drain()


def exchange_terms(rows_ref, terms_ref, gathered, received, send_sems, recv_sems, own_sems):
    place = Place()
    n_dp = terms_ref.shape[0]

    def peer(step):
        return lax.rem(place.dp + step, n_dp)

    others = [(peer(step), place.t) for step in range(1, n_dp)]
    greet(others + [place.at_y(1), place.at_y(-1), place.across(), place.sibling()])
    sends = Sends(send_sems, recv_sems)
    kept = [
        pltpu.make_async_copy(
            rows_ref.at[place.z], gathered.at[:, place.z, place.t], own_sems.at[0]
        ),
        pltpu.make_async_copy(
            terms_ref.at[place.dp], received.at[place.dp], own_sems.at[1]
        ),
    ]
    for copy in kept:
        copy.start()
    z_base = GROUP_KEYS

    def z_from(step):
        return lax.rem(place.z + step + NZ, NZ)

    for step in (1, 7, 2, 6, 3, 5, 4):
        sends.send(
            rows_ref.at[z_from(step)],
            gathered.at[:, place.z, place.t],
            z_base + step,
            place.at_z(step),
        )
    kv_base = z_base + NZ
    for step in range(1, n_dp):
        sends.send(
            terms_ref.at[peer(step)],
            received.at[place.dp],
            kv_base + step,
            (peer(step), place.t),
        )
    for step in range(1, NZ):
        sends.arrived(
            gathered.at[:, z_from(-step), place.t], z_base + step, place.at_z(-step)
        )
    kept[0].wait()

    def slot(block, half):
        return gathered.at[half, :, block]

    g = GroupGather(place, lambda half: slot(place.t, half), slot, sends, 0)
    g.start()
    for direction in (0, 1):
        g.take_y(0, direction, direction)
    g.take_x(0)
    for direction in (0, 1):
        g.take_y(0, 1 - direction, direction)
    g.take_x(1)
    for direction in (0, 1):
        g.take_far(0, direction)
    for half in (0, 1):
        for direction in (0, 1):
            g.take_y(1, half, direction)
    for direction in (0, 1):
        g.take_far(1, direction)
    g.take_shared()
    for step in range(1, n_dp):
        sends.arrived(
            received.at[peer(n_dp - step)], kv_base + step, (peer(n_dp - step), place.t)
        )
    kept[1].wait()
    sends.drain()


VMEM = pl.BlockSpec(memory_space=pltpu.VMEM)
ANY = pl.BlockSpec(memory_space=pl.ANY)


def on_device(hidden, connector, routing, talker_in, norm_gain, kv_weight, kv_grad):
    n_dp = lax.axis_size("dp")
    n_tensor = lax.axis_size("tensor")
    rows_dev, d_dev = hidden.shape
    capacity, width = talker_in.shape
    kv_width = kv_grad.shape[1]
    factor = 1.0 / math.sqrt(rows_dev * n_dp)
    slots = n_tensor * capacity
    bf16 = jnp.bfloat16

    first = 2 * GROUP_KEYS + 8
    talkers, kvs, hiddens = pl.pallas_call(
        gather_inputs,
        out_shape=(
            jax.ShapeDtypeStruct((n_tensor, capacity, width), bf16),
            jax.ShapeDtypeStruct((n_tensor, capacity, kv_width), bf16),
            jax.ShapeDtypeStruct((NZ, rows_dev, d_dev), bf16),
        ),
        in_specs=[VMEM] * 3,
        out_specs=[ANY] * 3,
        scratch_shapes=[
            pltpu.SemaphoreType.DMA((first,)),
            pltpu.SemaphoreType.DMA((first,)),
            pltpu.SemaphoreType.DMA((3,)),
        ],
        compiler_params=pltpu.CompilerParams(collective_id=0, has_side_effects=True),
    )(talker_in, kv_grad, hidden)

    route = routing[:, 0]
    shards = jnp.arange(n_tensor, dtype=jnp.int32)
    named = (route[:, None] == shards[None, :]).astype(jnp.float32)
    earlier = jnp.arange(rows_dev)[:, None] > jnp.arange(rows_dev)[None, :]
    before = jnp.dot(earlier.astype(jnp.float32), named, preferred_element_type=jnp.float32)
    ranks = jnp.sum(before * named, axis=1).astype(jnp.int32)
    slot_ids = route * capacity + ranks
    pick = (slot_ids[:, None] == jnp.arange(slots, dtype=jnp.int32)[None, :]).astype(bf16)

    talker_rows = jnp.dot(pick, talkers.reshape(slots, width), preferred_element_type=jnp.float32)
    kv_rows = jnp.dot(
        pick, kvs.reshape(slots, kv_width), preferred_element_type=jnp.float32
    ).astype(bf16)
    inv_rms = lax.rsqrt(jnp.mean(talker_rows * talker_rows, axis=1, keepdims=True) + 1e-06)
    scaled = talker_rows * inv_rms
    normed = (scaled * norm_gain).astype(bf16)
    back_grad = lax.dot_general(
        kv_rows, kv_weight, CONTRACT_LAST, preferred_element_type=jnp.float32
    )
    gain_back = norm_gain * back_grad
    row_grad = (
        inv_rms * (gain_back - scaled * jnp.mean(gain_back * scaled, axis=1, keepdims=True))
    ).astype(bf16)

    t = lax.axis_index("tensor")
    slice_rows = rows_dev // n_tensor
    own_rows = lax.dynamic_slice_in_dim(row_grad, t * slice_rows, slice_rows, 0)
    own_rows = own_rows.reshape(slice_rows, n_dp // NZ, NZ, width // n_dp).transpose(2, 1, 0, 3)
    per_dev = kv_width // (n_dp * n_tensor)
    own_cols = lax.dynamic_index_in_dim(
        kv_rows.reshape(rows_dev, n_dp, n_tensor, per_dev), t, 2, keepdims=False
    ).reshape(rows_dev, n_dp * per_dev)
    terms = lax.dot_general(own_cols, normed, CONTRACT_FIRST, preferred_element_type=jnp.float32)
    terms = (terms * factor).astype(bf16).reshape(n_dp, per_dev, width)

    second = GROUP_KEYS + NZ + n_dp
    gathered, received = pl.pallas_call(
        exchange_terms,
        out_shape=(
            jax.ShapeDtypeStruct((n_dp // NZ, NZ, n_tensor, slice_rows, width // n_dp), bf16),
            jax.ShapeDtypeStruct((n_dp, per_dev, width), bf16),
        ),
        in_specs=[VMEM] * 2,
        out_specs=[ANY] * 2,
        scratch_shapes=[
            pltpu.SemaphoreType.DMA((second,)),
            pltpu.SemaphoreType.DMA((second,)),
            pltpu.SemaphoreType.DMA((2,)),
        ],
        compiler_params=pltpu.CompilerParams(collective_id=1, has_side_effects=True),
    )(own_rows, terms)

    hidden_grad = lax.dot_general(
        row_grad, connector, CONTRACT_LAST, preferred_element_type=jnp.float32
    ).astype(bf16)
    kv_weight_grad = jnp.sum(received.astype(jnp.float32), axis=0).T
    all_hidden = hiddens.reshape(NZ * rows_dev, d_dev)
    blocks = gathered.reshape(n_dp // NZ, NZ * rows_dev, width // n_dp)
    x_lo = lax.axis_index("dp") // NZ

    def part(block):
        rows = lax.dynamic_index_in_dim(blocks, block, 0, keepdims=False)
        return (
            lax.dot_general(all_hidden, rows, CONTRACT_FIRST, preferred_element_type=jnp.float32)
            * factor
        )

    away = part(1 - x_lo).astype(bf16)
    swapped = lax.ppermute(away, "dp", [(i, (i + NZ) % (2 * NZ)) for i in range(2 * NZ)])
    connector_grad = part(x_lo) + swapped.astype(jnp.float32)
    return (hidden_grad, connector_grad, kv_weight_grad)


def solution(mesh):
    return jax.shard_map(
        on_device,
        mesh=mesh,
        in_specs=(
            P("dp", "tensor"),
            P("tensor", None),
            P("dp", None),
            P(("dp", "tensor"), None),
            P(),
            P(),
            P(("dp", "tensor"), None),
        ),
        out_specs=(P("dp", "tensor"), P("tensor", "dp"), P(None, ("dp", "tensor"))),
        check_vma=False,
    )
```

time: 196 us -> 108 us (0.55)
  the two profiles are of different devices: /device:TPU:8 before, /device:TPU:1 now
where the time goes in v1:
time: 108 us; the launch traced here: 107 us
  Pallas kernels  67.8 us (63%)
  matrix products  26.4 us (24%)
  other arithmetic  5.67 us (5%)
  waiting for transfers between devices  3.58 us (3%)
  local copies, waits for them, and re-layouts  2.19 us (2%)
    pallas_call x1, Pallas kernels, on_device(): pl.pallas_call(gather_inputs, out_shape=(jax.ShapeDtypeStruct((n_tensor,...  36.6 us
    pallas_call x1, Pallas kernels, on_device(): pl.pallas_call(exchange_terms, out_shape=(jax.ShapeDtypeStruct((n_dp // N...  31.3 us
    dot_general x1, matrix products, on_device(): lax.dot_general(kv_rows, kv_weight, CONTRACT_LAST, preferred_element_type...  8.25 us
    dot_general x2, matrix products, part(): lax.dot_general(all_hidden, rows, CONTRACT_FIRST, preferred_element_type=...  6.01 us
    dot_general x1, matrix products, on_device(): jnp.dot(pick, talkers.reshape(slots, width), preferred_element_type=jnp.f...  5.05 us
    convert_element_type x1, other arithmetic, on_device(): row_grad = (inv_rms * (gain_back - scaled * jnp.mean(gain_back * scaled,...  4.15 us
    ppermute x1, waiting for transfers between devices, on_device(): lax.ppermute(away, 'dp', [(i, (i + NZ) % (2 * NZ)) for i in range(2 * NZ)])  3.58 us
    dot_general x1, matrix products, on_device(): lax.dot_general(own_cols, normed, CONTRACT_FIRST, preferred_element_type=...  2.63 us
  transfers between devices with their start and end apart: 1, of which 1 were waited for; matrix products, arithmetic and copies ran while one was open for 2% of the time, Pallas kernels for 0%

profile of v1, /device:TPU:1, one launch (start us, length us, event | category | flops | bytes accessed | tf_op | source)
XLA Modules:
  0.0 107.5 jit_solution(11172900178930467083)
XLA Ops:
  0.6 1.0 fusion.4
  1.6 0.7 multiply_add_fusion
  2.3 36.6 %shard_map.94 = (bf16[16,32,3584]{2,1,0:T(8,128)(2,1)}, bf16[16,32,1024]{2,1,0:T(8,128)(2,1)}, bf16[8,256,512]{2,1,0:T(8,128)(2,1)}) custom-call(bf16[32,3584]{1,0:T(8,128)(2,1)} %talker_ref.1, bf16[32,1024]{1,0:T(8,128)(2,1)} %kv_ref.1, bf16[256,512]{1,0:T(8,128)(2,1)} %hidden_ref.1), custom_call_target="tpu_custom_call" | custom-call | tf_op jit(solution)/shard_map/pallas_call | solution.py:356
  38.9 1.7 %convolution_convert_fusion = bf16[256,1024]{1,0:T(8,128)(2,1)S(1)} fusion(bf16[512,1024]{1,0:T(8,128)(2,1)} %bitcast.32, s32[256]{0:T(256)S(1)} %bitcast.36), kind=kOutput, calls=%fused_computation.9 | convolution fusion | flops 268828672 | bytes 1573888 | tf_op jit(solution)/shard_map/dot_general | solution.py:383
  40.6 0.0 copy-start.1
  40.6 5.0 %multiply_reduce_fusion.1 = (f32[256]{0:T(256)S(1)}, f32[256,3584]{1,0:T(8,128)}) fusion(bf16[512,3584]{1,0:T(8,128)(2,1)} %bitcast.39, s32[256]{0:T(256)S(1)} %bitcast.37), kind=kOutput, calls=%fused_computation.6 | convolution fusion | flops 941489920 | bytes 7342080 | tf_op jit(solution)/shard_map/dot_general | solution.py:382
  45.7 0.2 copy.11
  45.9 0.1 reshape.56
  46.1 0.0 copy-done.1
  46.1 2.6 %fusion = bf16[64,3584]{1,0:T(8,128)(2,1)S(1)} fusion(bf16[256,64]{0,1:T(8,128)(2,1)S(1)} %reshape.57, f32[256,3584]{1,0:T(8,128)} %get-tuple-element.14, f32[3584]{0:T(1024)S(1)} %copy-done.1, f32[256]{0:T(256)S(1)} %add_rsqrt_fusion), kind=kOutput, calls=%fused_computation.2 | convolution fusion | flops 120651776 | bytes 4176896 | tf_op jit(solution)/shard_map/dot_general | solution.py:405
  48.7 0.9 reshape.58.terms_ref
  49.6 8.3 %multiply_reduce_fusion = (f32[256]{0:T(256)S(1)}, f32[256,3584]{1,0:T(8,128)}) fusion(f32[256,3584]{1,0:T(8,128)} %get-tuple-element.14, f32[256]{0:T(256)S(1)} %add_rsqrt_fusion, bf16[256,1024]{1,0:T(8,128)(2,1)S(1)} %convolution_convert_fusion, bf16[3584,1024]{1,0:T(8,128)(2,1)} %param.12, f32[3584]{0:T(1024)S(1)} %copy-done.1), kind=kOutput, calls=%fused_computation.5 | convolution fusion | flops 1882717952 | bytes 15220736 | tf_op jit(solution)/shard_map/dot_general | solution.py:389
  57.8 4.2 %multiply_convert_fusion.1 = bf16[256,3584]{1,0:T(8,128)(2,1)S(1)} fusion(f32[256,3584]{1,0:T(8,128)} %get-tuple-element.16, f32[256,3584]{1,0:T(8,128)} %get-tuple-element.14, f32[256]{0:T(256)S(1)} %broadcast_multiply_fusion, f32[256]{0:T(256)S(1)} %add_rsqrt_fusion), kind=kLoop, calls=%fused_computation.4 | loop fusion | flops 4587520 | bytes 9177088 | tf_op jit(solution)/shard_map/convert_element_type | solution.py:395
  62.0 0.2 reshape.55
  62.2 0.7 copy.13
  62.9 31.3 %shard_map.95 = (bf16[2,8,16,16,224]{4,3,2,1,0:T(8,128)(2,1)}, bf16[16,4,3584]{2,1,0:T(4,128)(2,1)}) custom-call(bf16[8,2,16,224]{3,2,1,0:T(8,128)(2,1)} %bitcast.33, bf16[16,4,3584]{2,1,0:T(4,128)(2,1)} %reshape.58.terms_ref), custom_call_target="tpu_custom_call" | custom-call | tf_op jit(solution)/shard_map/pallas_call | solution.py:409
  94.2 0.0 copy-start.2
  94.2 2.7 %fusion.3 = bf16[512,224]{0,1:T(8,128)(2,1)S(1)} fusion(bf16[2048,512]{1,0:T(8,128)(2,1)} %bitcast.40, bf16[2,2048,224]{2,1,0:T(8,128)(2,1)} %bitcast.42, s32[]{:T(128)S(6)} %select_n.23), kind=kOutput, calls=%fused_computation.13 | convolution fusion | flops 469991424 | bytes 3375108 | tf_op jit(solution)/shard_map/dot_general | solution.py:436
  96.9 0.0 copy-start
  96.9 1.0 collective-permute-start
  97.9 0.0 copy-done.2
  97.9 1.8 %convolution_convert_fusion.1 = bf16[256,512]{1,0:T(8,128)(2,1)} fusion(bf16[256,3584]{1,0:T(8,128)(2,1)S(1)} %multiply_convert_fusion.1, bf16[512,3584]{1,0:T(8,128)(2,1)S(1)} %copy-done.2), kind=kOutput, calls=%fused_computation.12 | convolution fusion | flops 939655168 | bytes 5767168 | tf_op jit(solution)/shard_map/dot_general | solution.py:425
  99.8 0.0 copy-done
  99.8 0.8 convert_reduce_fusion
  100.6 3.6 %collective-permute-done = bf16[512,224]{0,1:T(8,128)(2,1)S(1)} collective-permute-done((bf16[512,224]{0,1:T(8,128)(2,1)S(1)}, bf16[512,224]{0,1:T(8,128)(2,1)S(1)}, u32[]{:S(2)}, u32[]{:S(2)}) %collective-permute-start) | collective-permute-done | bytes 229408 | tf_op jit(solution)/shard_map/ppermute | solution.py:441
  104.1 3.3 %convert_add_fusion = f32[512,224]{0,1:T(8,128)} fusion(bf16[512,224]{0,1:T(8,128)(2,1)S(1)} %collective-permute-done, bf16[2048,512]{1,0:T(8,128)(2,1)} %bitcast.41, bf16[2,2048,224]{2,1,0:T(8,128)(2,1)} %bitcast.43, s32[]{:T(128)S(6)} %select_n.22), kind=kOutput, calls=%fused_computation.23 | convolution fusion | flops 470106112 | bytes 3833860 | tf_op jit(solution)/shard_map/dot_general | solution.py:436
  (6 shorter events, 0.1 us)
Async XLA Ops:
  40.6 5.5 %copy-start.1 = (f32[3584]{0:T(1024)S(1)}, f32[3584]{0:T(1024)}, u32[]{:S(2)}) copy-start(f32[3584]{0:T(1024)} %param.11) | copy-start | bytes 43012
  94.2 3.7 %copy-start.2 = (bf16[512,3584]{1,0:T(8,128)(2,1)S(1)}, bf16[512,3584]{1,0:T(8,128)(2,1)}, u32[]{:S(2)}) copy-start(bf16[512,3584]{1,0:T(8,128)(2,1)} %param.8) | copy-start | bytes 11010052
  96.9 2.8 %copy-start = (bf16[16,4,3584]{2,1,0:T(4,128)(2,1)S(1)}, bf16[16,4,3584]{2,1,0:T(4,128)(2,1)}, u32[]{:S(2)}) copy-start(bf16[16,4,3584]{2,1,0:T(4,128)(2,1)} %get-tuple-element.12) | copy-start | bytes 1376260
  96.9 7.2 %collective-permute-start = (bf16[512,224]{0,1:T(8,128)(2,1)S(1)}, bf16[512,224]{0,1:T(8,128)(2,1)S(1)}, u32[]{:S(2)}, u32[]{:S(2)}) collective-permute-start(bf16[512,224]{0,1:T(8,128)(2,1)S(1)} %fusion.3), channel_id=1, source_target_pairs={{0,128},{16,144},{32,160},{48,176},{64,192},{80,208},{96,224},{112... | collective-permute-start | bytes 688136 | tf_op jit(solution)/shard_map/ppermute | solution.py:441

commit v2 on v1

v2 whole, which is shorter than its diff:
```python
import math

import jax
import jax.numpy as jnp
from jax import lax
from jax.experimental import pallas as pl
from jax.experimental.pallas import tpu as pltpu
from jax.sharding import PartitionSpec as P

MESH = pl.DeviceIdType.MESH
CONTRACT_LAST = (((1,), (1,)), ((), ()))
CONTRACT_FIRST = (((0,), (0,)), ((), ()))

NZ = 8
NY = 4


class Place:
    def __init__(self):
        self.dp = lax.axis_index("dp")
        self.t = lax.axis_index("tensor")
        self.z = lax.rem(self.dp, NZ)
        self.xl = lax.div(self.dp, NZ)
        self.core = lax.rem(self.t, 2)
        self.y = lax.rem(lax.div(self.t, 2), NY)
        self.xh = lax.div(self.t, 2 * NY)

    def tensor(self, xh, y, core):
        return xh * (2 * NY) + lax.rem(y + NY, NY) * 2 + core

    def at_y(self, step):
        return (self.dp, self.tensor(self.xh, self.y + step, self.core))

    def at_z(self, step):
        return (self.xl * NZ + lax.rem(self.z + step + NZ, NZ), self.t)

    def across(self):
        return (self.dp, self.tensor(1 - self.xh, self.y, self.core))

    def sibling(self):
        return (self.dp, self.tensor(self.xh, self.y, 1 - self.core))


def greet(devices):
    barrier = pltpu.get_barrier_semaphore()
    for device in devices:
        pl.semaphore_signal(barrier, inc=1, device_id=device, device_id_type=MESH)
    pl.semaphore_wait(barrier, len(devices))


class Sends:
    def __init__(self, send_sems, recv_sems):
        self.send_sems, self.recv_sems = send_sems, recv_sems
        self.open = []

    def send(self, src, dst, key, device):
        copy = pltpu.make_async_remote_copy(
            src_ref=src,
            dst_ref=dst,
            send_sem=self.send_sems.at[key],
            recv_sem=self.recv_sems.at[key],
            device_id=device,
            device_id_type=MESH,
        )
        copy.start()
        self.open.append(copy)

    def arrived(self, dst, key, device):
        pltpu.make_async_remote_copy(
            src_ref=dst,
            dst_ref=dst,
            send_sem=self.send_sems.at[key],
            recv_sem=self.recv_sems.at[key],
            device_id=device,
            device_id_type=MESH,
        ).wait_recv()

    def drain(self):
        for copy in self.open:
            copy.wait_send()


GROUP_KEYS = 12 + 2 + 16


def key_y(direction, far, kind):
    return direction * 6 + far * 3 + kind


def key_x(half):
    return 12 + half


def key_s(hop, half):
    return 14 + hop * 2 + half


class GroupGather:
    def __init__(self, place, own, slot, sends, base):
        self.place, self.own, self.slot = place, own, slot
        self.sends, self.base = sends, base

    def block(self, far, step):
        p = self.place
        return p.tensor(1 - p.xh if far else p.xh, p.y + step, p.core)

    def twin(self, far, step):
        p = self.place
        return p.tensor(1 - p.xh if far else p.xh, p.y + step, 1 - p.core)

    def hop(self, far, step):
        return far * 4 + step % 4

    def share(self, src, far, step, half):
        self.sends.send(
            src,
            self.slot(self.block(far, step), half),
            self.base + key_s(self.hop(far, step), half),
            self.place.sibling(),
        )

    def to_y(self, src, far, half, direction):
        step = 1 if direction == 0 else -1
        self.sends.send(
            src,
            self.slot(self.block(far, 0), half),
            self.base + key_y(direction, far, half),
            self.place.at_y(step),
        )

    def start(self):
        for half in (0, 1):
            self.to_y(self.own(half), 0, half, 0)
            self.to_y(self.own(1 - half), 0, 1 - half, 1)
            self.sends.send(
                self.own(half),
                self.slot(self.block(0, 0), half),
                self.base + key_x(half),
                self.place.across(),
            )
        for half in (0, 1):
            self.share(self.own(half), 0, 0, half)

    def take_x(self, half):
        dst = self.slot(self.block(1, 0), half)
        self.sends.arrived(dst, self.base + key_x(half), self.place.across())
        self.to_y(dst, 1, half, 0)
        self.to_y(dst, 1, half, 1)
        self.share(dst, 1, 0, half)

    def take_y(self, far, half, direction):
        step = -1 if direction == 0 else 1
        dst = self.slot(self.block(far, step), half)
        self.sends.arrived(
            dst, self.base + key_y(direction, far, half), self.place.at_y(step)
        )
        if half == direction:
            self.sends.send(
                dst,
                dst,
                self.base + key_y(direction, far, 2),
                self.place.at_y(-step),
            )
        self.share(dst, far, step, half)

    def take_far(self, far, direction):
        step = -1 if direction == 0 else 1
        half = direction
        dst = self.slot(self.block(far, 2 * step), half)
        self.sends.arrived(
            dst, self.base + key_y(direction, far, 2), self.place.at_y(step)
        )
        self.share(dst, far, 2, half)

    def take_shared(self):
        for far in (0, 1):
            for step in (0, 1, 2, 3):
                for half in (0, 1):
                    self.sends.arrived(
                        self.slot(self.twin(far, step), half),
                        self.base + key_s(self.hop(far, step), half),
                        self.place.sibling(),
                    )


class GatherFromY(GroupGather):
    def start(self):
        for half in (0, 1):
            self.to_y(self.own(half), 0, half, 0)
            self.to_y(self.own(1 - half), 0, 1 - half, 1)
            self.to_x(self.own(half), 0, half)
        for half in (0, 1):
            self.share(self.own(half), 0, 0, half)

    def to_x(self, src, step, half):
        self.sends.send(
            src,
            self.slot(self.block(0, step), half),
            self.base + key_from_y(step, half),
            self.place.across(),
        )

    def take_y(self, far, half, direction):
        super().take_y(0, half, direction)
        step = -1 if direction == 0 else 1
        self.to_x(self.slot(self.block(0, step), half), step, half)

    def take_far(self, far, direction):
        super().take_far(0, direction)
        self.to_x(self.slot(self.block(0, 2), direction), 2, direction)

    def take_x(self, step, half):
        dst = self.slot(self.block(1, step), half)
        self.sends.arrived(dst, self.base + key_from_y(step, half), self.place.across())
        self.share(dst, 1, step, half)


def key_from_y(step, half):
    return (3, 4, 5, 9, 10, 11, 12, 13)[(step % 4) * 2 + half]


TILE = 512
BLOCK = 256
WINDOW = 384


def onehot(rows):
    return jnp.where(rows, 1.0, 0.0).astype(jnp.bfloat16)


def dot(a, b, contract):
    return lax.dot_general(a, b, (contract, ((), ())), preferred_element_type=jnp.float32)


NN = ((1,), (0,))
NT = ((1,), (1,))
TN = ((0,), (0,))


def whole(
    talker_ref, kv_ref, hidden_ref, gain_ref, ids_row_ref, ids_col_ref, weight_any, connector_any,
    hidden_grad_ref, connector_grad_ref, weight_grad_ref,
    talkers, kvs, hiddens, ids, weight, connector,
    local_back, local_grad, packed, blocks, ordered, pick, rows, kv_rows, back, columns, terms, terms_in,
    away, away_in, sums, sums_in, total, send_sems, recv_sems, own_sems,
):
    bf16, f32 = jnp.bfloat16, jnp.float32
    place = Place()
    width = talker_ref.shape[1]
    tiles = width // TILE
    capacity = talker_ref.shape[0]
    n_tensor = talkers.shape[0]
    slots = n_tensor * capacity
    rows_dev = hidden_ref.shape[0]
    factor = 1.0 / math.sqrt(rows_dev * 2 * NZ)
    loads = [
        pltpu.make_async_copy(weight_any, weight, own_sems.at[0]),
        pltpu.make_async_copy(connector_any, connector, own_sems.at[1]),
    ]
    for load in loads:
        load.start()
    over_x = (lax.rem(place.dp + NZ, 2 * NZ), place.t)
    greet(
        [place.at_z(step) for step in range(1, NZ)]
        + [place.at_y(1), place.at_y(-1), place.across(), place.sibling(), over_x]
    )
    sends = Sends(send_sems, recv_sems)
    half_rows = capacity // 2
    half_hidden = rows_dev // 2
    kept = [
        pltpu.make_async_copy(talker_ref, talkers.at[place.t], own_sems.at[2]),
        pltpu.make_async_copy(kv_ref, kvs.at[place.t], own_sems.at[3]),
        pltpu.make_async_copy(hidden_ref, hiddens.at[place.z], own_sems.at[4]),
        pltpu.make_async_copy(ids_row_ref, ids.at[place.z], own_sems.at[5]),
    ]

    def tile_of(i):
        return pl.ds(pl.multiple_of(i * TILE, TILE), TILE)

    def gather(own_ref, where, base):
        return GroupGather(
            place,
            lambda half: own_ref.at[pl.ds(half * half_rows, half_rows)],
            lambda block, half: where.at[block, pl.ds(half * half_rows, half_rows)],
            sends,
            base,
        )

    pair = (gather(talker_ref, talkers, 0), gather(kv_ref, kvs, GROUP_KEYS))

    def block_slot(block, half):
        return blocks.at[half, block]

    third = GatherFromY(
        place, lambda half: block_slot(place.t, half), block_slot, sends, 2 * GROUP_KEYS
    )
    z_base = 3 * GROUP_KEYS
    ids_base = z_base + NZ
    packed_base = ids_base + NZ
    terms_base = packed_base + NZ
    x_base = terms_base + NZ

    def z_at(step):
        return lax.rem(place.z + step + NZ, NZ)

    def z_slot(step, part=None):
        slot = hiddens.at[z_at(step)]
        if part is None:
            return slot
        return slot.at[pl.ds(part * half_hidden, half_hidden)]

    def pass_z(hop):
        for direction, step in ((0, -1), (1, 1)):
            if hop:
                sends.arrived(z_slot(hop * step), z_base + direction * 4 + hop - 1, place.at_z(step))
            part = direction if hop == 3 else None
            src = z_slot(hop * step, part) if hop else hidden_ref
            sends.send(
                src, z_slot(hop * step, part), z_base + direction * 4 + hop, place.at_z(-step)
            )

    def to_all_z(src, dst, base):
        for step in (1, 7, 2, 6, 3, 5, 4):
            sends.send(src(step), dst, base + step, place.at_z(step))

    def from_all_z(dst, base):
        for step in (1, 7, 2, 6, 3, 5, 4):
            sends.arrived(dst(-step), base + step, place.at_z(-step))

    def own_slots():
        def first(i, carry):
            squares, products = carry
            tile = tile_of(i)
            inputs = talker_ref[:, tile].astype(f32)
            gained = gain_ref[:, tile] * dot(kv_ref[...], weight[tile, :], NT)
            local_back[:, tile] = gained
            return (
                squares + jnp.sum(inputs * inputs, axis=1, keepdims=True),
                products + jnp.sum(gained * inputs, axis=1, keepdims=True),
            )

        zero = jnp.zeros((capacity, 1), f32)
        squares, products = lax.fori_loop(0, tiles, first, (zero, zero))
        inv_rms = lax.rsqrt(squares / width + 1e-06)
        mean = products * inv_rms / width

        def second(i, carry):
            tile = tile_of(i)
            scaled = talker_ref[:, tile].astype(f32) * inv_rms
            local_grad[:, tile] = (inv_rms * (local_back[:, tile] - scaled * mean)).astype(bf16)
            return carry

        lax.fori_loop(0, tiles, second, 0)
        piece = width // (2 * NZ)
        window_at = lax.broadcasted_iota(jnp.int32, (WINDOW, BLOCK), 0)
        wanted = lax.broadcasted_iota(jnp.int32, (WINDOW, BLOCK), 1)
        for index in range(2 * NZ):
            start = min(index * piece // 128 * 128, width - WINDOW)
            shift = onehot(
                (window_at == wanted + (index * piece - start)) & (wanted < piece)
            )
            packed[index % NZ, index // NZ] = dot(
                local_grad[:, start : start + WINDOW], shift, NN
            ).astype(bf16)

    def order_hidden(first, count):
        def one(i, carry):
            at = lax.rem(place.z + i + first + NZ, NZ)
            slot = lax.broadcasted_iota(jnp.int32, (slots, rows_dev), 0)
            chosen = onehot(slot == ids[at, 0:1, :])
            moved = dot(chosen, hiddens[at], NN).astype(bf16)
            for block in range(n_tensor):
                ordered[block, at] = moved[block * capacity : (block + 1) * capacity]
            return carry

        lax.fori_loop(0, count, one, 0)

    def pick_rows():
        slot = lax.broadcasted_iota(jnp.int32, (rows_dev, slots), 1)
        pick[...] = onehot(ids_col_ref[...] == slot)
        kv_all = kvs[...].reshape(slots, kvs.shape[2])
        kv_rows[...] = dot(pick[...], kv_all, NN).astype(bf16)
        at = lax.broadcasted_iota(jnp.int32, columns_shape, 0)
        col = lax.broadcasted_iota(jnp.int32, columns_shape, 1)
        dp = ((at >> 2) & 1) * NZ + (at >> 3)
        chosen = onehot(col == (dp * n_tensor + place.t) * 4 + (at & 3))
        columns[...] = dot(chosen, kv_rows[...], NT).astype(bf16)

        def one(i, squares):
            tile = tile_of(i)
            inputs = dot(pick[...], talkers[:, :, tile].reshape(slots, TILE), NN)
            rows[:, tile] = inputs.astype(bf16)
            return squares + jnp.sum(inputs * inputs, axis=1, keepdims=True)

        squares = lax.fori_loop(0, tiles, one, jnp.zeros((rows_dev, 1), f32))
        return lax.rsqrt(squares / width + 1e-06)

    columns_shape = (terms.shape[0] * terms.shape[1], kv_ref.shape[1])

    def make_terms(inv_rms):
        def one(i, carry):
            tile = tile_of(i)
            normed = ((rows[:, tile].astype(f32) * inv_rms) * gain_ref[:, tile]).astype(bf16)
            term = dot(columns[...], normed, NN)
            for at in range(NZ):
                terms[at, :, tile] = term[at * 8 : (at + 1) * 8].astype(bf16)
            return carry

        lax.fori_loop(0, tiles, one, 0)

    def make_back(first, last, products):
        def one(i, products):
            tile = tile_of(i)
            gained = gain_ref[:, tile] * dot(kv_rows[...], weight[tile, :], NT)
            back[:, tile] = gained
            return products + jnp.sum(gained * rows[:, tile].astype(f32), axis=1, keepdims=True)

        return lax.fori_loop(first, last, one, products)

    def make_hidden_grad(inv_rms, products):
        mean = products * inv_rms / width
        total[...] = jnp.zeros_like(total)

        def one(i, carry):
            tile = tile_of(i)
            scaled = rows[:, tile].astype(f32) * inv_rms
            grad = (inv_rms * (back[:, tile] - scaled * mean)).astype(bf16)
            total[...] += dot(grad, connector[:, tile], NT)
            return carry

        lax.fori_loop(0, tiles, one, 0)
        hidden_grad_ref[...] = total[...].astype(bf16)

    def connector_part(block, first):
        part = n_tensor // 4

        def piece(i):
            at = pl.ds(first + i * part, part)
            lhs = blocks[block, at].reshape(part * NZ * capacity, BLOCK)
            rhs = ordered[at].reshape(part * NZ * capacity, ordered.shape[3])
            return dot(lhs, rhs, TN)

        return piece(0) + piece(1)

    for g in pair:
        g.start()
    pass_z(0)
    to_all_z(lambda step: ids_row_ref, ids.at[place.z], ids_base)
    for copy in kept:
        copy.start()
    loads[0].wait()
    own_slots()
    own_packed = pltpu.make_async_copy(
        packed.at[place.z], blocks.at[:, place.t, place.z], own_sems.at[6]
    )
    own_packed.start()
    to_all_z(lambda step: packed.at[z_at(step)], blocks.at[:, place.t, place.z], packed_base)
    for direction in (0, 1):
        for g in pair:
            g.take_y(0, direction, direction)
    for g in pair:
        g.take_x(0)
    for direction in (0, 1):
        for g in pair:
            g.take_y(0, 1 - direction, direction)
    for g in pair:
        g.take_x(1)
    pass_z(1)
    for direction in (0, 1):
        for g in pair:
            g.take_far(0, direction)
    from_all_z(lambda step: ids.at[z_at(step)], ids_base)
    kept[2].wait()
    kept[3].wait()
    order_hidden(-1, 3)
    from_all_z(lambda step: blocks.at[:, place.t, z_at(step)], packed_base)
    own_packed.wait()
    third.start()
    for half in (0, 1):
        for direction in (0, 1):
            for g in pair:
                g.take_y(1, half, direction)
    for direction in (0, 1):
        third.take_y(0, direction, direction)
    for direction in (0, 1):
        for g in pair:
            g.take_far(1, direction)
    pass_z(2)
    for g in pair:
        g.take_shared()
    kept[0].wait()
    kept[1].wait()
    inv_rms = pick_rows()
    for direction in (0, 1):
        third.take_y(0, 1 - direction, direction)
    for direction in (0, 1):
        third.take_far(0, direction)
    make_terms(inv_rms)
    to_all_z(lambda step: terms.at[z_at(step)], terms_in.at[place.z], terms_base)
    pass_z(3)
    products = make_back(0, 4, jnp.zeros((rows_dev, 1), f32))
    for half in (0, 1):
        third.take_x(0, half)
    products = make_back(4, tiles, products)
    order_hidden(2, 2)
    order_hidden(-3, 2)
    for half in (0, 1):
        third.take_x(1, half)
        third.take_x(-1, half)
    loads[1].wait()
    make_hidden_grad(inv_rms, products)
    for half in (0, 1):
        third.take_x(2, half)
    for direction, step in ((0, -1), (1, 1)):
        sends.arrived(z_slot(4 * step, direction), z_base + direction * 4 + 3, place.at_z(step))
    order_hidden(4, 1)
    third.take_shared()
    near = place.xh * (n_tensor // 2)
    far = (1 - place.xh) * (n_tensor // 2)
    away[...] = (connector_part(1 - place.xl, near) + connector_part(1 - place.xl, far)).astype(bf16)
    sends.send(away, away_in, x_base, over_x)
    from_all_z(lambda step: terms_in.at[z_at(step)], terms_base)
    terms_in[place.z] = terms[place.z]

    def add_up(i, carry):
        tile = tile_of(i)
        sums[:, tile] = jnp.sum(terms_in[:, :, tile].astype(f32), axis=0)
        return carry

    lax.fori_loop(0, tiles, add_up, 0)
    sends.send(sums, sums_in, x_base + 1, over_x)
    total[...] = connector_part(place.xl, near) + connector_part(place.xl, far)
    sends.arrived(sums_in, x_base + 1, over_x)
    both = sums[...] + sums_in[...]
    weight_grad_ref[...] = jnp.where(place.xl == 0, both[0:4], both[4:8]) * factor
    sends.arrived(away_in, x_base, over_x)
    out_rows = connector_grad_ref.shape[0]
    connector_grad_ref[...] = (
        total[0:out_rows, :] + away_in[0:out_rows, :].astype(f32)
    ) * factor
    sends.drain()


VMEM = pl.BlockSpec(memory_space=pltpu.VMEM)
ANY = pl.BlockSpec(memory_space=pl.ANY)


def on_device(hidden, connector, routing, talker_in, norm_gain, kv_weight, kv_grad):
    n_dp = lax.axis_size("dp")
    n_tensor = lax.axis_size("tensor")
    rows_dev, d_dev = hidden.shape
    capacity, width = talker_in.shape
    kv_width = kv_grad.shape[1]
    slots = n_tensor * capacity
    per_dev = kv_width // (n_dp * n_tensor)
    bf16, f32 = jnp.bfloat16, jnp.float32

    route = routing[:, 0]
    shards = jnp.arange(n_tensor, dtype=jnp.int32)
    named = (route[:, None] == shards[None, :]).astype(f32)
    earlier = jnp.arange(rows_dev)[:, None] > jnp.arange(rows_dev)[None, :]
    before = jnp.dot(earlier.astype(f32), named, preferred_element_type=f32)
    ranks = jnp.sum(before * named, axis=1).astype(jnp.int32)
    slot_ids = route * capacity + ranks

    keys = 3 * GROUP_KEYS + 4 * NZ + 2
    hidden_grad, connector_grad, weight_grad = pl.pallas_call(
        whole,
        out_shape=(
            jax.ShapeDtypeStruct((rows_dev, d_dev), bf16),
            jax.ShapeDtypeStruct((width // n_dp, d_dev), f32),
            jax.ShapeDtypeStruct((per_dev, width), f32),
        ),
        in_specs=[VMEM] * 6 + [ANY] * 2,
        out_specs=[VMEM] * 3,
        scratch_shapes=[
            pltpu.VMEM((n_tensor, capacity, width), bf16),
            pltpu.VMEM((n_tensor, capacity, kv_width), bf16),
            pltpu.VMEM((NZ, rows_dev, d_dev), bf16),
            pltpu.VMEM((NZ, 8, rows_dev), jnp.int32),
            pltpu.VMEM(kv_weight.shape, bf16),
            pltpu.VMEM(connector.shape, bf16),
            pltpu.VMEM((capacity, width), f32),
            pltpu.VMEM((capacity, width), bf16),
            pltpu.VMEM((NZ, 2, capacity, BLOCK), bf16),
            pltpu.VMEM((2, n_tensor, NZ, capacity, BLOCK), bf16),
            pltpu.VMEM((n_tensor, NZ, capacity, d_dev), bf16),
            pltpu.VMEM((rows_dev, slots), bf16),
            pltpu.VMEM((rows_dev, width), bf16),
            pltpu.VMEM((rows_dev, kv_width), bf16),
            pltpu.VMEM((rows_dev, width), f32),
            pltpu.VMEM((n_dp * per_dev, rows_dev), bf16),
            pltpu.VMEM((NZ, 8, width), bf16),
            pltpu.VMEM((NZ, 8, width), bf16),
            pltpu.VMEM((BLOCK, d_dev), bf16),
            pltpu.VMEM((BLOCK, d_dev), bf16),
            pltpu.VMEM((8, width), f32),
            pltpu.VMEM((8, width), f32),
            pltpu.VMEM((BLOCK, d_dev), f32),
            pltpu.SemaphoreType.DMA((keys,)),
            pltpu.SemaphoreType.DMA((keys,)),
            pltpu.SemaphoreType.DMA((7,)),
        ],
        compiler_params=pltpu.CompilerParams(
            collective_id=0, has_side_effects=True, vmem_limit_bytes=60 * 1024 * 1024
        ),
    )(
        talker_in,
        kv_grad,
        hidden,
        norm_gain[None, :],
        jnp.broadcast_to(slot_ids[None, :], (8, rows_dev)),
        slot_ids[:, None],
        kv_weight,
        connector,
    )
    return (hidden_grad, connector_grad.T, weight_grad.T)


def solution(mesh):
    return jax.shard_map(
        on_device,
        mesh=mesh,
        in_specs=(
            P("dp", "tensor"),
            P("tensor", None),
            P("dp", None),
            P(("dp", "tensor"), None),
            P(),
            P(),
            P(("dp", "tensor"), None),
        ),
        out_specs=(P("dp", "tensor"), P("tensor", "dp"), P(None, ("dp", "tensor"))),
        check_vma=False,
    )
```

time: 108 us -> 85.1 us (0.79)
  matrix products: 26.4 us -> 0.95 us
  Pallas kernels: 67.8 us -> 74.1 us
  local copies, waits for them, and re-layouts: 2.19 us -> 7.65 us
  other arithmetic: 5.67 us -> 1.37 us
  waiting for transfers between devices: 3.58 us -> 0 us
    dot_general x8 -> x1, matrix products: 26.4 us -> 0.95 us  [on_device(): before = jnp.dot(earlier.astype(f32), named, preferred_element_type=f32)]
    pallas_call x2 -> x1, Pallas kernels: 67.8 us -> 74.1 us  [on_device(): pl.pallas_call(whole, out_shape=(jax.ShapeDtypeStruct((rows_dev, d_dev),...]
    unnamed x6 -> x3, local copies, waits for them, and re-layouts: 0.02 us -> 4.93 us
    convert_element_type x1 -> x0, other arithmetic: 4.15 us -> none  [on_device(): row_grad = (inv_rms * (gain_back - scaled * jnp.mean(gain_back * scaled,...]
    ppermute x1 -> x0, waiting for transfers between devices: 3.58 us -> none  [on_device(): lax.ppermute(away, 'dp', [(i, (i + NZ) % (2 * NZ)) for i in range(2 * NZ)])]
    broadcast_in_dim x0 -> x2, local copies, waits for them, and re-layouts: none -> 1.93 us  [the longest x1 1.33 us: on_device(): norm_gain[None, :]]
    reshape x5 -> x0, local copies, waits for them, and re-layouts: 1.92 us -> none  [the longest x2 0.9 us: on_device(): own_rows.reshape(slice_rows, n_dp // NZ, NZ, width // n_dp)]
  transfers between devices with their start and end apart: 1 -> 0, of which waited for: 1 -> 0; matrix products, arithmetic and copies ran while one was open for 2% -> 0% of each run, Pallas kernels for 0% -> 0%
where the time goes in v2:
time: 85.1 us; the launch traced here: 84.7 us
  Pallas kernels  74.1 us (87%)
  local copies, waits for them, and re-layouts  7.65 us (9%)
  other arithmetic  1.37 us (2%)
  matrix products  0.95 us (1%)
    pallas_call x1, Pallas kernels, on_device(): pl.pallas_call(whole, out_shape=(jax.ShapeDtypeStruct((rows_dev, d_dev),...  74.1 us
    unnamed x3, local copies, waits for them, and re-layouts  4.93 us

profile of v2, /device:TPU:1, one launch (start us, length us, event | category | flops | bytes accessed | tf_op | source)
XLA Modules:
  0.0 84.7 jit_solution(13049549786691134760)
XLA Ops:
  0.6 1.0 %fusion = f32[256]{0:T(256)S(1)} fusion(s32[256]{0:T(256)} %bitcast.6), kind=kOutput, calls=%fused_computation.1 | convolution fusion | flops 2178816 | bytes 2048 | tf_op jit(solution)/shard_map/dot_general | solution.py:562
  1.6 0.7 multiply_add_fusion.1
  2.3 0.7 multiply_add_fusion
  3.0 0.6 broadcast_in_dim.5.ids_row_ref
  3.6 1.3 %broadcast_in_dim.4.gain_ref = f32[1,3584]{1,0:T(1,128)} reshape(f32[3584]{0:T(1024)} %param.11) | data formatting | bytes 28672 | tf_op jit(solution)/shard_map/broadcast_in_dim | solution.py:611
  4.9 0.8 copy.15.ids_col_ref
  5.7 74.1 %shard_map.94 = (bf16[256,512]{1,0:T(8,128)(2,1)}, f32[224,512]{1,0:T(8,128)}, f32[4,3584]{1,0:T(4,128)}) custom-call(bf16[32,3584]{1,0:T(8,128)(2,1)} %talker_ref.1, bf16[32,1024]{1,0:T(8,128)(2,1)} %kv_ref.1, bf16[256,512]{1,0:T(8,128)(2,1)} %hidden_ref.1, f32[1,3584]{1,0:T(1,128)} %broadcast_in_dim.4.gain_ref, s32[8,256]{1,0:T(8,128)} %broadcast_in_dim.5.ids_row_ref, ...), custom_call_target="tpu_custom_call" | custom-call | tf_op jit(solution)/shard_map/pallas_call | solution.py:567
  79.8 1.7 %copy.19 = bf16[256,512]{1,0:T(8,128)(2,1)} copy(bf16[256,512]{1,0:T(8,128)(2,1)} %get-tuple-element.12) | data formatting | bytes 524288
  81.5 1.8 %copy.20 = f32[512,224]{0,1:T(8,128)} copy(f32[512,224]{0,1:T(8,128)} %bitcast.4) | data formatting | bytes 917504
  83.3 1.4 %copy.21 = f32[3584,4]{0,1:T(4,128)} copy(f32[3584,4]{0,1:T(4,128)} %bitcast.5) | data formatting | bytes 114688
  (1 shorter events, 0.0 us)

commit v3 on v2

--- a/solution.py
+++ b/solution.py
@@ -1,3 +1,4 @@
+import functools
 import math
 
 import jax
@@ -130,8 +131,8 @@
 
     def start(self):
         for half in (0, 1):
-            self.to_y(self.own(half), 0, half, 0)
-            self.to_y(self.own(1 - half), 0, 1 - half, 1)
+            self.to_y(self.own(half), 0, half, half)
+            self.to_y(self.own(half), 0, half, 1 - half)
             self.sends.send(
                 self.own(half),
                 self.slot(self.block(0, 0), half),
@@ -172,10 +173,10 @@
         )
         self.share(dst, far, 2, half)
 
-    def take_shared(self):
+    def take_shared(self, halves=(0, 1)):
         for far in (0, 1):
             for step in (0, 1, 2, 3):
-                for half in (0, 1):
+                for half in halves:
                     self.sends.arrived(
                         self.slot(self.twin(far, step), half),
                         self.base + key_s(self.hop(far, step), half),
@@ -238,11 +239,11 @@
 
 
 def whole(
-    talker_ref, kv_ref, hidden_ref, gain_ref, ids_row_ref, ids_col_ref, weight_any, connector_any,
-    hidden_grad_ref, connector_grad_ref, weight_grad_ref,
+    talker_ref, kv_ref, hidden_ref, gain_rows_ref, route_ref, weight_any, connector_any,
+    hidden_grad_ref, own_sum_ref, swapped_ref, weight_sums_ref,
     talkers, kvs, hiddens, ids, weight, connector,
     local_back, local_grad, packed, blocks, ordered, pick, rows, kv_rows, back, columns, terms, terms_in,
-    away, away_in, sums, sums_in, total, send_sems, recv_sems, own_sems,
+    away, away_in, sums, sums_in, total, gain_ref, own_ids, send_sems, recv_sems, own_sems,
 ):
     bf16, f32 = jnp.bfloat16, jnp.float32
     place = Place()
@@ -252,7 +253,7 @@
     n_tensor = talkers.shape[0]
     slots = n_tensor * capacity
     rows_dev = hidden_ref.shape[0]
-    factor = 1.0 / math.sqrt(rows_dev * 2 * NZ)
+    piece_rows = own_sum_ref.shape[0]
     loads = [
         pltpu.make_async_copy(weight_any, weight, own_sems.at[0]),
         pltpu.make_async_copy(connector_any, connector, own_sems.at[1]),
@@ -271,14 +272,13 @@
         pltpu.make_async_copy(talker_ref, talkers.at[place.t], own_sems.at[2]),
         pltpu.make_async_copy(kv_ref, kvs.at[place.t], own_sems.at[3]),
         pltpu.make_async_copy(hidden_ref, hiddens.at[place.z], own_sems.at[4]),
-        pltpu.make_async_copy(ids_row_ref, ids.at[place.z], own_sems.at[5]),
     ]
 
     def tile_of(i):
         return pl.ds(pl.multiple_of(i * TILE, TILE), TILE)
 
     def gather(own_ref, where, base):
-        return GroupGather(
+        return GatherFromY(
             place,
             lambda half: own_ref.at[pl.ds(half * half_rows, half_rows)],
             lambda block, half: where.at[block, pl.ds(half * half_rows, half_rows)],
@@ -289,9 +289,9 @@
     pair = (gather(talker_ref, talkers, 0), gather(kv_ref, kvs, GROUP_KEYS))
 
     def block_slot(block, half):
-        return blocks.at[half, block]
-
-    third = GatherFromY(
+        return blocks.at[lax.rem(1 - place.xl + half, 2), block]
+
+    third = GroupGather(
         place, lambda half: block_slot(place.t, half), block_slot, sends, 2 * GROUP_KEYS
     )
     z_base = 3 * GROUP_KEYS
@@ -326,6 +326,22 @@
     def from_all_z(dst, base):
         for step in (1, 7, 2, 6, 3, 5, 4):
             sends.arrived(dst(-step), base + step, place.at_z(-step))
+
+    def number_rows():
+        route = route_ref[...]
+        shard = lax.broadcasted_iota(jnp.int32, (n_tensor, rows_dev), 0)
+        named = shard == route
+        earlier = lax.broadcasted_iota(jnp.int32, (rows_dev, rows_dev), 0)
+        later = lax.broadcasted_iota(jnp.int32, (rows_dev, rows_dev), 1)
+        before = dot(onehot(named), onehot(earlier < later), NN)
+        rank = jnp.sum(jnp.where(named, before, 0.0), axis=0, keepdims=True)
+        slot = route * capacity + rank.astype(jnp.int32)
+        slot = jnp.broadcast_to(slot, own_ids.shape)
+        own_ids[...] = slot
+        ids[place.z] = slot
+        lanes = gain_rows_ref.shape[1]
+        for i in range(gain_rows_ref.shape[0]):
+            gain_ref[:, i * lanes : (i + 1) * lanes] = gain_rows_ref[i : i + 1, :]
 
     def own_slots():
         def first(i, carry):
@@ -376,8 +392,11 @@
         lax.fori_loop(0, count, one, 0)
 
     def pick_rows():
-        slot = lax.broadcasted_iota(jnp.int32, (rows_dev, slots), 1)
-        pick[...] = onehot(ids_col_ref[...] == slot)
+        slot = lax.broadcasted_iota(jnp.int32, (slots, rows_dev), 0)
+        chosen = onehot(slot == own_ids[0:1, :])
+        one = lax.broadcasted_iota(jnp.int32, (rows_dev, rows_dev), 0)
+        two = lax.broadcasted_iota(jnp.int32, (rows_dev, rows_dev), 1)
+        pick[...] = dot(onehot(one == two), chosen, NT).astype(bf16)
         kv_all = kvs[...].reshape(slots, kvs.shape[2])
         kv_rows[...] = dot(pick[...], kv_all, NN).astype(bf16)
         at = lax.broadcasted_iota(jnp.int32, columns_shape, 0)
@@ -442,83 +461,74 @@
 
         return piece(0) + piece(1)
 
-    for g in pair:
-        g.start()
+    def both(step):
+        for g in pair:
+            step(g)
+
+    both(lambda g: g.start())
     pass_z(0)
-    to_all_z(lambda step: ids_row_ref, ids.at[place.z], ids_base)
     for copy in kept:
         copy.start()
+    number_rows()
+    to_all_z(lambda step: own_ids, ids.at[place.z], ids_base)
     loads[0].wait()
     own_slots()
     own_packed = pltpu.make_async_copy(
-        packed.at[place.z], blocks.at[:, place.t, place.z], own_sems.at[6]
+        packed.at[place.z], blocks.at[:, place.t, place.z], own_sems.at[5]
     )
     own_packed.start()
     to_all_z(lambda step: packed.at[z_at(step)], blocks.at[:, place.t, place.z], packed_base)
     for direction in (0, 1):
-        for g in pair:
-            g.take_y(0, direction, direction)
-    for g in pair:
-        g.take_x(0)
+        both(lambda g: g.take_y(0, direction, direction))
     for direction in (0, 1):
-        for g in pair:
-            g.take_y(0, 1 - direction, direction)
-    for g in pair:
-        g.take_x(1)
+        both(lambda g: g.take_y(0, 1 - direction, direction))
     pass_z(1)
+    for half in (0, 1):
+        both(lambda g: g.take_x(0, half))
     for direction in (0, 1):
-        for g in pair:
-            g.take_far(0, direction)
+        both(lambda g: g.take_far(0, direction))
     from_all_z(lambda step: ids.at[z_at(step)], ids_base)
     kept[2].wait()
-    kept[3].wait()
     order_hidden(-1, 3)
     from_all_z(lambda step: blocks.at[:, place.t, z_at(step)], packed_base)
     own_packed.wait()
     third.start()
+    pass_z(2)
+    for step in (1, -1):
+        for half in (0, 1):
+            both(lambda g: g.take_x(step, half))
     for half in (0, 1):
-        for direction in (0, 1):
-            for g in pair:
-                g.take_y(1, half, direction)
-    for direction in (0, 1):
-        third.take_y(0, direction, direction)
-    for direction in (0, 1):
-        for g in pair:
-            g.take_far(1, direction)
-    pass_z(2)
-    for g in pair:
-        g.take_shared()
+        third.take_y(0, half, half)
+        third.take_y(0, half, 1 - half)
+        third.take_x(half)
+    for half in (0, 1):
+        both(lambda g: g.take_x(2, half))
+    both(lambda g: g.take_shared())
     kept[0].wait()
     kept[1].wait()
     inv_rms = pick_rows()
-    for direction in (0, 1):
-        third.take_y(0, 1 - direction, direction)
-    for direction in (0, 1):
-        third.take_far(0, direction)
     make_terms(inv_rms)
     to_all_z(lambda step: terms.at[z_at(step)], terms_in.at[place.z], terms_base)
     pass_z(3)
-    products = make_back(0, 4, jnp.zeros((rows_dev, 1), f32))
     for half in (0, 1):
-        third.take_x(0, half)
-    products = make_back(4, tiles, products)
-    order_hidden(2, 2)
-    order_hidden(-3, 2)
-    for half in (0, 1):
-        third.take_x(1, half)
-        third.take_x(-1, half)
-    loads[1].wait()
-    make_hidden_grad(inv_rms, products)
-    for half in (0, 1):
-        third.take_x(2, half)
+        third.take_far(0, half)
+        third.take_y(1, half, half)
+        third.take_y(1, half, 1 - half)
+    products = make_back(0, tiles, jnp.zeros((rows_dev, 1), f32))
+    third.take_far(1, 0)
     for direction, step in ((0, -1), (1, 1)):
         sends.arrived(z_slot(4 * step, direction), z_base + direction * 4 + 3, place.at_z(step))
-    order_hidden(4, 1)
-    third.take_shared()
+    order_hidden(2, 5)
+    third.take_shared((0,))
     near = place.xh * (n_tensor // 2)
     far = (1 - place.xh) * (n_tensor // 2)
     away[...] = (connector_part(1 - place.xl, near) + connector_part(1 - place.xl, far)).astype(bf16)
-    sends.send(away, away_in, x_base, over_x)
+    third.take_far(1, 1)
+    sends.send(
+        away.at[pl.ds(0, piece_rows)], away_in.at[pl.ds(0, piece_rows)], x_base, over_x
+    )
+    loads[1].wait()
+    make_hidden_grad(inv_rms, products)
     from_all_z(lambda step: terms_in.at[z_at(step)], terms_base)
     terms_in[place.z] = terms[place.z]
 
@@ -528,17 +538,23 @@
         return carry
 
     lax.fori_loop(0, tiles, add_up, 0)
+    third.take_shared((1,))
     sends.send(sums, sums_in, x_base + 1, over_x)
     total[...] = connector_part(place.xl, near) + connector_part(place.xl, far)
+    own_sum_ref[...] = total[0:piece_rows, :]
     sends.arrived(sums_in, x_base + 1, over_x)
-    both = sums[...] + sums_in[...]
-    weight_grad_ref[...] = jnp.where(place.xl == 0, both[0:4], both[4:8]) * factor
-    sends.arrived(away_in, x_base, over_x)
-    out_rows = connector_grad_ref.shape[0]
-    connector_grad_ref[...] = (
-        total[0:out_rows, :] + away_in[0:out_rows, :].astype(f32)
-    ) * factor
+    weight_sums_ref[...] = sums[...] + sums_in[...]
+    sends.arrived(away_in.at[pl.ds(0, piece_rows)], x_base, over_x)
+    swapped_ref[...] = away_in[0:piece_rows, :]
     sends.drain()
+
+
+def close(factor, hidden_ref, own_ref, swapped_ref, sums_ref, hidden_grad_ref, connector_grad_ref, weight_grad_ref):
+    hidden_grad_ref[...] = hidden_ref[...]
+    connector_grad_ref[...] = (own_ref[...] + swapped_ref[...].astype(jnp.float32)) * factor
+    sums = sums_ref[...]
+    mine = jnp.where(lax.axis_index("dp") < NZ, sums[0:4], sums[4:8])
+    weight_grad_ref[...] = mine * factor
 
 
 VMEM = pl.BlockSpec(memory_space=pltpu.VMEM)
@@ -555,24 +571,17 @@
     per_dev = kv_width // (n_dp * n_tensor)
     bf16, f32 = jnp.bfloat16, jnp.float32
 
-    route = routing[:, 0]
-    shards = jnp.arange(n_tensor, dtype=jnp.int32)
-    named = (route[:, None] == shards[None, :]).astype(f32)
-    earlier = jnp.arange(rows_dev)[:, None] > jnp.arange(rows_dev)[None, :]
-    before = jnp.dot(earlier.astype(f32), named, preferred_element_type=f32)
-    ranks = jnp.sum(before * named, axis=1).astype(jnp.int32)
-    slot_ids = route * capacity + ranks
-
     keys = 3 * GROUP_KEYS + 4 * NZ + 2
-    hidden_grad, connector_grad, weight_grad = pl.pallas_call(
+    hidden_rows, own_sum, swapped, weight_sums = pl.pallas_call(
         whole,
         out_shape=(
             jax.ShapeDtypeStruct((rows_dev, d_dev), bf16),
             jax.ShapeDtypeStruct((width // n_dp, d_dev), f32),
-            jax.ShapeDtypeStruct((per_dev, width), f32),
+            jax.ShapeDtypeStruct((width // n_dp, d_dev), bf16),
+            jax.ShapeDtypeStruct((8, width), f32),
         ),
-        in_specs=[VMEM] * 6 + [ANY] * 2,
-        out_specs=[VMEM] * 3,
+        in_specs=[VMEM] * 5 + [ANY] * 2,
+        out_specs=[VMEM] * 4,
         scratch_shapes=[
             pltpu.VMEM((n_tensor, capacity, width), bf16),
             pltpu.VMEM((n_tensor, capacity, kv_width), bf16),
@@ -597,9 +606,11 @@
             pltpu.VMEM((8, width), f32),
             pltpu.VMEM((8, width), f32),
             pltpu.VMEM((BLOCK, d_dev), f32),
+            pltpu.VMEM((1, width), f32),
+            pltpu.VMEM((8, rows_dev), jnp.int32),
             pltpu.SemaphoreType.DMA((keys,)),
             pltpu.SemaphoreType.DMA((keys,)),
-            pltpu.SemaphoreType.DMA((7,)),
+            pltpu.SemaphoreType.DMA((6,)),
         ],
         compiler_params=pltpu.CompilerParams(
             collective_id=0, has_side_effects=True, vmem_limit_bytes=60 * 1024 * 1024
@@ -608,12 +619,22 @@
         talker_in,
         kv_grad,
         hidden,
-        norm_gain[None, :],
-        jnp.broadcast_to(slot_ids[None, :], (8, rows_dev)),
-        slot_ids[:, None],
+        norm_gain.reshape(width // 128, 128),
+        routing.T,
         kv_weight,
         connector,
     )
+    factor = 1.0 / math.sqrt(rows_dev * n_dp)
+    hidden_grad, connector_grad, weight_grad = pl.pallas_call(
+        functools.partial(close, factor),
+        out_shape=(
+            jax.ShapeDtypeStruct((rows_dev, d_dev), bf16),
+            jax.ShapeDtypeStruct((width // n_dp, d_dev), f32),
+            jax.ShapeDtypeStruct((per_dev, width), f32),
+        ),
+        in_specs=[VMEM] * 4,
+        out_specs=[VMEM] * 3,
+    )(hidden_rows, own_sum, swapped, weight_sums)
     return (hidden_grad, connector_grad.T, weight_grad.T)
 
 

time: 85.1 us -> 82.7 us (0.972)
  Pallas kernels: 74.1 us -> 81.9 us
  local copies, waits for them, and re-layouts: 7.65 us -> 0 us
  other arithmetic: 1.37 us -> 0 us
  matrix products: 0.95 us -> 0 us
    pallas_call x1, Pallas kernels: 74.1 us -> 79.8 us  [on_device(): pl.pallas_call(whole, out_shape=(jax.ShapeDtypeStruct((rows_dev, d_dev),...]
    unnamed x3 -> x0, local copies, waits for them, and re-layouts: 4.93 us -> none
    pallas_call x0 -> x1, Pallas kernels: none -> 2.1 us  [on_device(): pl.pallas_call(functools.partial(close, factor), out_shape=(jax.ShapeDtyp...]
    broadcast_in_dim x2 -> x0, local copies, waits for them, and re-layouts: 1.93 us -> none  [the longest x1 1.33 us: on_device(): norm_gain[None, :]]
    add x2 -> x0, other arithmetic: 1.37 us -> none  [on_device(): slot_ids = route * capacity + ranks]
    dot_general x1 -> x0, matrix products: 0.95 us -> none  [on_device(): before = jnp.dot(earlier.astype(f32), named, preferred_element_type=f32)]
where the time goes in v3:
time: 82.7 us; the launch traced here: 82.5 us
  Pallas kernels  81.9 us (99%)
    pallas_call x1, Pallas kernels, on_device(): pl.pallas_call(whole, out_shape=(jax.ShapeDtypeStruct((rows_dev, d_dev),...  79.8 us
    pallas_call x1, Pallas kernels, on_device(): pl.pallas_call(functools.partial(close, factor), out_shape=(jax.ShapeDtyp...  2.1 us

profile of v3, /device:TPU:1, one launch (start us, length us, event | category | flops | bytes accessed | tf_op | source)
XLA Modules:
  0.0 82.5 jit_solution(1536128306157309631)
XLA Ops:
  0.6 79.8 %shard_map.94 = (bf16[256,512]{1,0:T(8,128)(2,1)}, f32[224,512]{1,0:T(8,128)}, bf16[224,512]{1,0:T(8,128)(2,1)}, f32[8,3584]{1,0:T(8,128)}) custom-call(bf16[32,3584]{1,0:T(8,128)(2,1)} %talker_ref.1, bf16[32,1024]{1,0:T(8,128)(2,1)} %kv_ref.1, bf16[256,512]{1,0:T(8,128)(2,1)} %hidden_ref.1, f32[28,128]{1,0:T(8,128)} %bitcast.4, s32[1,256]{1,0:T(1,128)} %bitcast.5, ...), custom_call_target="tpu_custom_call" | custom-call | tf_op jit(solution)/shard_map/pallas_call | solution.py:575
  80.4 2.1 %shard_map.95 = (bf16[256,512]{1,0:T(8,128)(2,1)}, f32[224,512]{1,0:T(8,128)}, f32[4,3584]{1,0:T(4,128)}) custom-call(bf16[256,512]{1,0:T(8,128)(2,1)} %get-tuple-element.10.hidden_ref, f32[224,512]{1,0:T(8,128)} %get-tuple-element.11.own_ref, bf16[224,512]{1,0:T(8,128)(2,1)} %get-tuple-element.12.swapped_ref, f32[8,3584]{1,0:T(8,128)} %get-tuple-element.13.sums_ref), custom_call_target="tpu_custom_call" | custom-call | tf_op jit(solution)/shard_map/pallas_call | solution.py:628

commit v4 on v3

--- a/solution.py
+++ b/solution.py
@@ -129,18 +129,21 @@
             self.place.at_y(step),
         )
 
-    def start(self):
-        for half in (0, 1):
+    def start(self, halves=(0, 1)):
+        for half in halves:
             self.to_y(self.own(half), 0, half, half)
             self.to_y(self.own(half), 0, half, 1 - half)
-            self.sends.send(
-                self.own(half),
-                self.slot(self.block(0, 0), half),
-                self.base + key_x(half),
-                self.place.across(),
-            )
-        for half in (0, 1):
+            self.across_first(half)
+        for half in halves:
             self.share(self.own(half), 0, 0, half)
+
+    def across_first(self, half):
+        self.sends.send(
+            self.own(half),
+            self.slot(self.block(0, 0), half),
+            self.base + key_x(half),
+            self.place.across(),
+        )
 
     def take_x(self, half):
         dst = self.slot(self.block(1, 0), half)
@@ -185,13 +188,8 @@
 
 
 class GatherFromY(GroupGather):
-    def start(self):
-        for half in (0, 1):
-            self.to_y(self.own(half), 0, half, 0)
-            self.to_y(self.own(1 - half), 0, 1 - half, 1)
-            self.to_x(self.own(half), 0, half)
-        for half in (0, 1):
-            self.share(self.own(half), 0, 0, half)
+    def across_first(self, half):
+        self.to_x(self.own(half), 0, half)
 
     def to_x(self, src, step, half):
         self.sends.send(
@@ -241,9 +239,9 @@
 def whole(
     talker_ref, kv_ref, hidden_ref, gain_rows_ref, route_ref, weight_any, connector_any,
     hidden_grad_ref, own_sum_ref, swapped_ref, weight_sums_ref,
-    talkers, kvs, hiddens, ids, weight, connector,
-    local_back, local_grad, packed, blocks, ordered, pick, rows, kv_rows, back, columns, terms, terms_in,
-    away, away_in, sums, sums_in, total, gain_ref, own_ids, send_sems, recv_sems, own_sems,
+    talkers, kvs, hiddens, weight, connector,
+    local_rows, local_back, local_grad, packed, blocks, pick, rows, kv_rows, back, columns, terms, terms_in,
+    away, away_in, sums, sums_in, total, gain_ref, send_sems, recv_sems, own_sems,
 ):
     bf16, f32 = jnp.bfloat16, jnp.float32
     place = Place()
@@ -253,6 +251,7 @@
     n_tensor = talkers.shape[0]
     slots = n_tensor * capacity
     rows_dev = hidden_ref.shape[0]
+    share = rows_dev // n_tensor
     piece_rows = own_sum_ref.shape[0]
     loads = [
         pltpu.make_async_copy(weight_any, weight, own_sems.at[0]),
@@ -277,8 +276,8 @@
     def tile_of(i):
         return pl.ds(pl.multiple_of(i * TILE, TILE), TILE)
 
-    def gather(own_ref, where, base):
-        return GatherFromY(
+    def gather(kind, own_ref, where, base):
+        return kind(
             place,
             lambda half: own_ref.at[pl.ds(half * half_rows, half_rows)],
             lambda block, half: where.at[block, pl.ds(half * half_rows, half_rows)],
@@ -286,17 +285,19 @@
             base,
         )
 
-    pair = (gather(talker_ref, talkers, 0), gather(kv_ref, kvs, GROUP_KEYS))
+    wide = gather(GroupGather, talker_ref, talkers, 0)
+    thin = gather(GatherFromY, kv_ref, kvs, GROUP_KEYS)
 
     def block_slot(block, half):
-        return blocks.at[lax.rem(1 - place.xl + half, 2), block]
-
-    third = GroupGather(
-        place, lambda half: block_slot(place.t, half), block_slot, sends, 2 * GROUP_KEYS
-    )
-    z_base = 3 * GROUP_KEYS
-    ids_base = z_base + NZ
-    packed_base = ids_base + NZ
+        return blocks.at[lax.rem(1 - place.xl + half, 2), :, block]
+
+    def own_block(half):
+        return block_slot(place.t, half)
+
+    theirs = GroupGather(place, own_block, block_slot, sends, 2 * GROUP_KEYS)
+    ours = GatherFromY(place, own_block, block_slot, sends, 3 * GROUP_KEYS)
+    z_base = 4 * GROUP_KEYS
+    packed_base = z_base + NZ
     terms_base = packed_base + NZ
     x_base = terms_base + NZ
 
@@ -336,33 +337,38 @@
         before = dot(onehot(named), onehot(earlier < later), NN)
         rank = jnp.sum(jnp.where(named, before, 0.0), axis=0, keepdims=True)
         slot = route * capacity + rank.astype(jnp.int32)
-        slot = jnp.broadcast_to(slot, own_ids.shape)
-        own_ids[...] = slot
-        ids[place.z] = slot
+        slot_at = lax.broadcasted_iota(jnp.int32, (slots, rows_dev), 0)
+        same = onehot(earlier == later)
+        pick[...] = dot(same, onehot(slot_at == slot), NT).astype(bf16)
         lanes = gain_rows_ref.shape[1]
         for i in range(gain_rows_ref.shape[0]):
             gain_ref[:, i * lanes : (i + 1) * lanes] = gain_rows_ref[i : i + 1, :]
 
-    def own_slots():
+    def own_rows():
+        mine = pl.ds(pl.multiple_of(place.t * share, share), share)
+        kv_all = kvs[...].reshape(slots, kvs.shape[2])
+        kv_rows[...] = dot(pick[...], kv_all, NN).astype(bf16)
+
         def first(i, carry):
             squares, products = carry
             tile = tile_of(i)
-            inputs = talker_ref[:, tile].astype(f32)
-            gained = gain_ref[:, tile] * dot(kv_ref[...], weight[tile, :], NT)
+            inputs = dot(pick[mine, :], talkers[:, :, tile].reshape(slots, TILE), NN)
+            local_rows[:, tile] = inputs
+            gained = gain_ref[:, tile] * dot(kv_rows[mine, :], weight[tile, :], NT)
             local_back[:, tile] = gained
             return (
                 squares + jnp.sum(inputs * inputs, axis=1, keepdims=True),
                 products + jnp.sum(gained * inputs, axis=1, keepdims=True),
             )
 
-        zero = jnp.zeros((capacity, 1), f32)
+        zero = jnp.zeros((share, 1), f32)
         squares, products = lax.fori_loop(0, tiles, first, (zero, zero))
         inv_rms = lax.rsqrt(squares / width + 1e-06)
         mean = products * inv_rms / width
 
         def second(i, carry):
             tile = tile_of(i)
-            scaled = talker_ref[:, tile].astype(f32) * inv_rms
+            scaled = local_rows[:, tile] * inv_rms
             local_grad[:, tile] = (inv_rms * (local_back[:, tile] - scaled * mean)).astype(bf16)
             return carry
 
@@ -379,26 +385,7 @@
                 local_grad[:, start : start + WINDOW], shift, NN
             ).astype(bf16)
 
-    def order_hidden(first, count):
-        def one(i, carry):
-            at = lax.rem(place.z + i + first + NZ, NZ)
-            slot = lax.broadcasted_iota(jnp.int32, (slots, rows_dev), 0)
-            chosen = onehot(slot == ids[at, 0:1, :])
-            moved = dot(chosen, hiddens[at], NN).astype(bf16)
-            for block in range(n_tensor):
-                ordered[block, at] = moved[block * capacity : (block + 1) * capacity]
-            return carry
-
-        lax.fori_loop(0, count, one, 0)
-
     def pick_rows():
-        slot = lax.broadcasted_iota(jnp.int32, (slots, rows_dev), 0)
-        chosen = onehot(slot == own_ids[0:1, :])
-        one = lax.broadcasted_iota(jnp.int32, (rows_dev, rows_dev), 0)
-        two = lax.broadcasted_iota(jnp.int32, (rows_dev, rows_dev), 1)
-        pick[...] = dot(onehot(one == two), chosen, NT).astype(bf16)
-        kv_all = kvs[...].reshape(slots, kvs.shape[2])
-        kv_rows[...] = dot(pick[...], kv_all, NN).astype(bf16)
         at = lax.broadcasted_iota(jnp.int32, columns_shape, 0)
         col = lax.broadcasted_iota(jnp.int32, columns_shape, 1)
         dp = ((at >> 2) & 1) * NZ + (at >> 3)
@@ -450,85 +437,90 @@
         lax.fori_loop(0, tiles, one, 0)
         hidden_grad_ref[...] = total[...].astype(bf16)
 
-    def connector_part(block, first):
-        part = n_tensor // 4
-
-        def piece(i):
-            at = pl.ds(first + i * part, part)
-            lhs = blocks[block, at].reshape(part * NZ * capacity, BLOCK)
-            rhs = ordered[at].reshape(part * NZ * capacity, ordered.shape[3])
-            return dot(lhs, rhs, TN)
-
-        return piece(0) + piece(1)
-
-    def both(step):
-        for g in pair:
-            step(g)
-
-    both(lambda g: g.start())
+    def connector_part(block):
+        part = NZ // 4
+        total[...] = jnp.zeros_like(total)
+
+        def one(i, carry):
+            at = pl.ds(i * part, part)
+            lhs = blocks[block, at].reshape(part * rows_dev, BLOCK)
+            rhs = hiddens[at].reshape(part * rows_dev, hiddens.shape[2])
+            total[...] += dot(lhs, rhs, TN)
+            return carry
+
+        lax.fori_loop(0, 4, one, 0)
+
+    wide.start()
+    thin.start()
     pass_z(0)
     for copy in kept:
         copy.start()
     number_rows()
-    to_all_z(lambda step: own_ids, ids.at[place.z], ids_base)
+    for direction in (0, 1):
+        wide.take_y(0, direction, direction)
+    wide.take_x(0)
+    for direction in (0, 1):
+        wide.take_y(0, 1 - direction, direction)
+    wide.take_x(1)
+    pass_z(1)
+    for half in (0, 1):
+        for direction in (half, 1 - half):
+            thin.take_y(0, half, direction)
+    for direction in (0, 1):
+        wide.take_far(0, direction)
+        thin.take_far(0, direction)
+    for direction in (0, 1):
+        wide.take_y(1, direction, direction)
+    pass_z(2)
+    for direction in (0, 1):
+        wide.take_y(1, 1 - direction, direction)
+    for step in (0, 1, -1, 2):
+        for half in (0, 1):
+            thin.take_x(step, half)
+    for direction in (0, 1):
+        wide.take_far(1, direction)
+    thin.take_shared()
+    wide.take_shared()
+    kept[0].wait()
+    kept[1].wait()
     loads[0].wait()
-    own_slots()
+    own_rows()
     own_packed = pltpu.make_async_copy(
-        packed.at[place.z], blocks.at[:, place.t, place.z], own_sems.at[5]
+        packed.at[place.z], blocks.at[:, place.z, place.t], own_sems.at[5]
     )
     own_packed.start()
-    to_all_z(lambda step: packed.at[z_at(step)], blocks.at[:, place.t, place.z], packed_base)
-    for direction in (0, 1):
-        both(lambda g: g.take_y(0, direction, direction))
-    for direction in (0, 1):
-        both(lambda g: g.take_y(0, 1 - direction, direction))
-    pass_z(1)
-    for half in (0, 1):
-        both(lambda g: g.take_x(0, half))
-    for direction in (0, 1):
-        both(lambda g: g.take_far(0, direction))
-    from_all_z(lambda step: ids.at[z_at(step)], ids_base)
-    kept[2].wait()
-    order_hidden(-1, 3)
-    from_all_z(lambda step: blocks.at[:, place.t, z_at(step)], packed_base)
-    own_packed.wait()
-    third.start()
-    pass_z(2)
-    for step in (1, -1):
-        for half in (0, 1):
-            both(lambda g: g.take_x(step, half))
-    for half in (0, 1):
-        third.take_y(0, half, half)
-        third.take_y(0, half, 1 - half)
-        third.take_x(half)
-    for half in (0, 1):
-        both(lambda g: g.take_x(2, half))
-    both(lambda g: g.take_shared())
-    kept[0].wait()
-    kept[1].wait()
+    to_all_z(lambda step: packed.at[z_at(step)], blocks.at[:, place.z, place.t], packed_base)
+    pass_z(3)
     inv_rms = pick_rows()
     make_terms(inv_rms)
+    from_all_z(lambda step: blocks.at[:, z_at(step), place.t], packed_base)
+    own_packed.wait()
+    theirs.start((0,))
     to_all_z(lambda step: terms.at[z_at(step)], terms_in.at[place.z], terms_base)
-    pass_z(3)
-    for half in (0, 1):
-        third.take_far(0, half)
-        third.take_y(1, half, half)
-        third.take_y(1, half, 1 - half)
     products = make_back(0, tiles, jnp.zeros((rows_dev, 1), f32))
-    third.take_far(1, 0)
+    theirs.take_x(0)
+    ours.start((1,))
+    theirs.take_y(0, 0, 0)
+    theirs.take_y(0, 0, 1)
+    theirs.take_far(0, 0)
+    theirs.take_y(1, 0, 0)
+    theirs.take_y(1, 0, 1)
+    ours.take_x(0, 1)
+    ours.take_y(0, 1, 1)
+    ours.take_y(0, 1, 0)
+    theirs.take_far(1, 0)
+    ours.take_far(0, 1)
     for direction, step in ((0, -1), (1, 1)):
         sends.arrived(z_slot(4 * step, direction), z_base + direction * 4 + 3, place.at_z(step))
-    order_hidden(2, 5)
-    third.take_shared((0,))
-    near = place.xh * (n_tensor // 2)
-    far = (1 - place.xh) * (n_tensor // 2)
-    away[...] = (connector_part(1 - place.xl, near) + connector_part(1 - place.xl, far)).astype(bf16)
-    third.take_far(1, 1)
+    kept[2].wait()
+    theirs.take_shared((0,))
+    connector_part(1 - place.xl)
+    away[...] = total[...].astype(bf16)
+    for step in (1, -1):
+        ours.take_x(step, 1)
     sends.send(
         away.at[pl.ds(0, piece_rows)], away_in.at[pl.ds(0, piece_rows)], x_base, over_x
     )
-    loads[1].wait()
-    make_hidden_grad(inv_rms, products)
     from_all_z(lambda step: terms_in.at[z_at(step)], terms_base)
     terms_in[place.z] = terms[place.z]
 
@@ -538,9 +530,12 @@
         return carry
 
     lax.fori_loop(0, tiles, add_up, 0)
-    third.take_shared((1,))
     sends.send(sums, sums_in, x_base + 1, over_x)
-    total[...] = connector_part(place.xl, near) + connector_part(place.xl, far)
+    loads[1].wait()
+    make_hidden_grad(inv_rms, products)
+    ours.take_x(2, 1)
+    ours.take_shared((1,))
+    connector_part(place.xl)
     own_sum_ref[...] = total[0:piece_rows, :]
     sends.arrived(sums_in, x_base + 1, over_x)
     weight_sums_ref[...] = sums[...] + sums_in[...]
@@ -568,10 +563,11 @@
     capacity, width = talker_in.shape
     kv_width = kv_grad.shape[1]
     slots = n_tensor * capacity
+    share = rows_dev // n_tensor
     per_dev = kv_width // (n_dp * n_tensor)
     bf16, f32 = jnp.bfloat16, jnp.float32
 
-    keys = 3 * GROUP_KEYS + 4 * NZ + 2
+    keys = 4 * GROUP_KEYS + 3 * NZ + 2
     hidden_rows, own_sum, swapped, weight_sums = pl.pallas_call(
         whole,
         out_shape=(
@@ -586,14 +582,13 @@
             pltpu.VMEM((n_tensor, capacity, width), bf16),
             pltpu.VMEM((n_tensor, capacity, kv_width), bf16),
             pltpu.VMEM((NZ, rows_dev, d_dev), bf16),
-            pltpu.VMEM((NZ, 8, rows_dev), jnp.int32),
             pltpu.VMEM(kv_weight.shape, bf16),
             pltpu.VMEM(connector.shape, bf16),
-            pltpu.VMEM((capacity, width), f32),
-            pltpu.VMEM((capacity, width), bf16),
-            pltpu.VMEM((NZ, 2, capacity, BLOCK), bf16),
-            pltpu.VMEM((2, n_tensor, NZ, capacity, BLOCK), bf16),
-            pltpu.VMEM((n_tensor, NZ, capacity, d_dev), bf16),
+            pltpu.VMEM((share, width), f32),
+            pltpu.VMEM((share, width), f32),
+            pltpu.VMEM((share, width), bf16),
+            pltpu.VMEM((NZ, 2, share, BLOCK), bf16),
+            pltpu.VMEM((2, NZ, n_tensor, share, BLOCK), bf16),
             pltpu.VMEM((rows_dev, slots), bf16),
             pltpu.VMEM((rows_dev, width), bf16),
             pltpu.VMEM((rows_dev, kv_width), bf16),
@@ -607,7 +602,6 @@
             pltpu.VMEM((8, width), f32),
             pltpu.VMEM((BLOCK, d_dev), f32),
             pltpu.VMEM((1, width), f32),
-            pltpu.VMEM((8, rows_dev), jnp.int32),
             pltpu.SemaphoreType.DMA((keys,)),
             pltpu.SemaphoreType.DMA((keys,)),
             pltpu.SemaphoreType.DMA((6,)),

time: 82.7 us -> 73.6 us (0.89)
  Pallas kernels: 81.9 us -> 72.2 us
    pallas_call x1, Pallas kernels: 79.8 us -> 70.1 us  [on_device(): pl.pallas_call(whole, out_shape=(jax.ShapeDtypeStruct((rows_dev, d_dev),...]
where the time goes in v4:
time: 73.6 us; the launch traced here: 72.8 us
  Pallas kernels  72.2 us (98%)
    pallas_call x1, Pallas kernels, on_device(): pl.pallas_call(whole, out_shape=(jax.ShapeDtypeStruct((rows_dev, d_dev),...  70.1 us
    pallas_call x1, Pallas kernels, on_device(): pl.pallas_call(functools.partial(close, factor), out_shape=(jax.ShapeDtyp...  2.1 us

profile of v4, /device:TPU:1, one launch (start us, length us, event | category | flops | bytes accessed | tf_op | source)
XLA Modules:
  0.0 72.8 jit_solution(9335446816872883898)
XLA Ops:
  0.6 70.1 %shard_map.94 = (bf16[256,512]{1,0:T(8,128)(2,1)}, f32[224,512]{1,0:T(8,128)}, bf16[224,512]{1,0:T(8,128)(2,1)}, f32[8,3584]{1,0:T(8,128)}) custom-call(bf16[32,3584]{1,0:T(8,128)(2,1)} %talker_ref.1, bf16[32,1024]{1,0:T(8,128)(2,1)} %kv_ref.1, bf16[256,512]{1,0:T(8,128)(2,1)} %hidden_ref.1, f32[28,128]{1,0:T(8,128)} %bitcast.4, s32[1,256]{1,0:T(1,128)} %bitcast.5, ...), custom_call_target="tpu_custom_call" | custom-call | tf_op jit(solution)/shard_map/pallas_call | solution.py:571
  70.7 2.1 %shard_map.95 = (bf16[256,512]{1,0:T(8,128)(2,1)}, f32[224,512]{1,0:T(8,128)}, f32[4,3584]{1,0:T(4,128)}) custom-call(bf16[256,512]{1,0:T(8,128)(2,1)} %get-tuple-element.10.hidden_ref, f32[224,512]{1,0:T(8,128)} %get-tuple-element.11.own_ref, bf16[224,512]{1,0:T(8,128)(2,1)} %get-tuple-element.12.swapped_ref, f32[8,3584]{1,0:T(8,128)} %get-tuple-element.13.sums_ref), custom_call_target="tpu_custom_call" | custom-call | tf_op jit(solution)/shard_map/pallas_call | solution.py:622

commit v5 on v4

--- a/solution.py
+++ b/solution.py
@@ -240,8 +240,8 @@
     talker_ref, kv_ref, hidden_ref, gain_rows_ref, route_ref, weight_any, connector_any,
     hidden_grad_ref, own_sum_ref, swapped_ref, weight_sums_ref,
     talkers, kvs, hiddens, weight, connector,
-    local_rows, local_back, local_grad, packed, blocks, pick, rows, kv_rows, back, columns, terms, terms_in,
-    away, away_in, sums, sums_in, total, gain_ref, send_sems, recv_sems, own_sems,
+    local_rows, local_back, local_grad, packed, blocks, shifts, pick, rows, kv_rows, back, columns, terms, terms_in,
+    away, away_in, sums, sums_out, sums_in, total, gain_ref, send_sems, recv_sems, own_sems,
 ):
     bf16, f32 = jnp.bfloat16, jnp.float32
     place = Place()
@@ -373,17 +373,17 @@
             return carry
 
         lax.fori_loop(0, tiles, second, 0)
-        piece = width // (2 * NZ)
+        for index in range(2 * NZ):
+            start, kind = cuts[index]
+            packed[index % NZ, index // NZ] = dot(
+                local_grad[:, start : start + WINDOW], shifts[kind], NN
+            ).astype(bf16)
+
+    def make_shifts():
         window_at = lax.broadcasted_iota(jnp.int32, (WINDOW, BLOCK), 0)
         wanted = lax.broadcasted_iota(jnp.int32, (WINDOW, BLOCK), 1)
-        for index in range(2 * NZ):
-            start = min(index * piece // 128 * 128, width - WINDOW)
-            shift = onehot(
-                (window_at == wanted + (index * piece - start)) & (wanted < piece)
-            )
-            packed[index % NZ, index // NZ] = dot(
-                local_grad[:, start : start + WINDOW], shift, NN
-            ).astype(bf16)
+        for kind, offset in enumerate(offsets):
+            shifts[kind] = onehot((window_at == wanted + offset) & (wanted < piece))
 
     def pick_rows():
         at = lax.broadcasted_iota(jnp.int32, columns_shape, 0)
@@ -401,6 +401,10 @@
         squares = lax.fori_loop(0, tiles, one, jnp.zeros((rows_dev, 1), f32))
         return lax.rsqrt(squares / width + 1e-06)
 
+    piece = width // (2 * NZ)
+    starts = [min(i * piece // 128 * 128, width - WINDOW) for i in range(2 * NZ)]
+    offsets = sorted({i * piece - start for i, start in enumerate(starts)})
+    cuts = [(start, offsets.index(i * piece - start)) for i, start in enumerate(starts)]
     columns_shape = (terms.shape[0] * terms.shape[1], kv_ref.shape[1])
 
     def make_terms(inv_rms):
@@ -456,6 +460,7 @@
     for copy in kept:
         copy.start()
     number_rows()
+    make_shifts()
     for direction in (0, 1):
         wide.take_y(0, direction, direction)
     wide.take_x(0)
@@ -496,28 +501,29 @@
     from_all_z(lambda step: blocks.at[:, z_at(step), place.t], packed_base)
     own_packed.wait()
     theirs.start((0,))
+    ours.start((1,))
     to_all_z(lambda step: terms.at[z_at(step)], terms_in.at[place.z], terms_base)
     products = make_back(0, tiles, jnp.zeros((rows_dev, 1), f32))
+    ours.take_y(0, 1, 1)
+    theirs.take_y(0, 0, 0)
+    ours.take_y(0, 1, 0)
+    theirs.take_y(0, 0, 1)
     theirs.take_x(0)
-    ours.start((1,))
-    theirs.take_y(0, 0, 0)
-    theirs.take_y(0, 0, 1)
+    ours.take_far(0, 1)
+    ours.take_x(0, 1)
     theirs.take_far(0, 0)
     theirs.take_y(1, 0, 0)
     theirs.take_y(1, 0, 1)
-    ours.take_x(0, 1)
-    ours.take_y(0, 1, 1)
-    ours.take_y(0, 1, 0)
+    for step in (1, -1):
+        ours.take_x(step, 1)
     theirs.take_far(1, 0)
-    ours.take_far(0, 1)
+    ours.take_x(2, 1)
     for direction, step in ((0, -1), (1, 1)):
         sends.arrived(z_slot(4 * step, direction), z_base + direction * 4 + 3, place.at_z(step))
     kept[2].wait()
     theirs.take_shared((0,))
     connector_part(1 - place.xl)
     away[...] = total[...].astype(bf16)
-    for step in (1, -1):
-        ours.take_x(step, 1)
     sends.send(
         away.at[pl.ds(0, piece_rows)], away_in.at[pl.ds(0, piece_rows)], x_base, over_x
     )
@@ -526,19 +532,20 @@
 
     def add_up(i, carry):
         tile = tile_of(i)
-        sums[:, tile] = jnp.sum(terms_in[:, :, tile].astype(f32), axis=0)
+        added = jnp.sum(terms_in[:, :, tile].astype(f32), axis=0)
+        sums[:, tile] = added
+        sums_out[:, tile] = added.astype(bf16)
         return carry
 
     lax.fori_loop(0, tiles, add_up, 0)
-    sends.send(sums, sums_in, x_base + 1, over_x)
+    sends.send(sums_out, sums_in, x_base + 1, over_x)
     loads[1].wait()
     make_hidden_grad(inv_rms, products)
-    ours.take_x(2, 1)
     ours.take_shared((1,))
     connector_part(place.xl)
     own_sum_ref[...] = total[0:piece_rows, :]
     sends.arrived(sums_in, x_base + 1, over_x)
-    weight_sums_ref[...] = sums[...] + sums_in[...]
+    weight_sums_ref[...] = sums[...] + sums_in[...].astype(f32)
     sends.arrived(away_in.at[pl.ds(0, piece_rows)], x_base, over_x)
     swapped_ref[...] = away_in[0:piece_rows, :]
     sends.drain()
@@ -589,6 +596,7 @@
             pltpu.VMEM((share, width), bf16),
             pltpu.VMEM((NZ, 2, share, BLOCK), bf16),
             pltpu.VMEM((2, NZ, n_tensor, share, BLOCK), bf16),
+            pltpu.VMEM((8, WINDOW, BLOCK), bf16),
             pltpu.VMEM((rows_dev, slots), bf16),
             pltpu.VMEM((rows_dev, width), bf16),
             pltpu.VMEM((rows_dev, kv_width), bf16),
@@ -599,7 +607,8 @@
             pltpu.VMEM((BLOCK, d_dev), bf16),
             pltpu.VMEM((BLOCK, d_dev), bf16),
             pltpu.VMEM((8, width), f32),
-            pltpu.VMEM((8, width), f32),
+            pltpu.VMEM((8, width), bf16),
+            pltpu.VMEM((8, width), bf16),
             pltpu.VMEM((BLOCK, d_dev), f32),
             pltpu.VMEM((1, width), f32),
             pltpu.SemaphoreType.DMA((keys,)),

time: 73.6 us -> 72.5 us (0.985)
  no operation moved by 1% of the time
where the time goes in v5:
time: 72.5 us; the launch traced here: 72.3 us
  Pallas kernels  71.7 us (99%)
    pallas_call x1, Pallas kernels, on_device(): pl.pallas_call(whole, out_shape=(jax.ShapeDtypeStruct((rows_dev, d_dev),...  69.6 us
    pallas_call x1, Pallas kernels, on_device(): pl.pallas_call(functools.partial(close, factor), out_shape=(jax.ShapeDtyp...  2.1 us

profile of v5, /device:TPU:1, one launch (start us, length us, event | category | flops | bytes accessed | tf_op | source)
XLA Modules:
  0.0 72.3 jit_solution(11517948181475551253)
XLA Ops:
  0.6 69.6 %shard_map.94 = (bf16[256,512]{1,0:T(8,128)(2,1)}, f32[224,512]{1,0:T(8,128)}, bf16[224,512]{1,0:T(8,128)(2,1)}, f32[8,3584]{1,0:T(8,128)}) custom-call(bf16[32,3584]{1,0:T(8,128)(2,1)} %talker_ref.1, bf16[32,1024]{1,0:T(8,128)(2,1)} %kv_ref.1, bf16[256,512]{1,0:T(8,128)(2,1)} %hidden_ref.1, f32[28,128]{1,0:T(8,128)} %bitcast.4, s32[1,256]{1,0:T(1,128)} %bitcast.5, ...), custom_call_target="tpu_custom_call" | custom-call | tf_op jit(solution)/shard_map/pallas_call | solution.py:578
  70.2 2.1 %shard_map.95 = (bf16[256,512]{1,0:T(8,128)(2,1)}, f32[224,512]{1,0:T(8,128)}, f32[4,3584]{1,0:T(4,128)}) custom-call(bf16[256,512]{1,0:T(8,128)(2,1)} %get-tuple-element.10.hidden_ref, f32[224,512]{1,0:T(8,128)} %get-tuple-element.11.own_ref, bf16[224,512]{1,0:T(8,128)(2,1)} %get-tuple-element.12.swapped_ref, f32[8,3584]{1,0:T(8,128)} %get-tuple-element.13.sums_ref), custom_call_target="tpu_custom_call" | custom-call | tf_op jit(solution)/shard_map/pallas_call | solution.py:631

commit v6 on v5

--- a/solution.py
+++ b/solution.py
@@ -240,7 +240,7 @@
     talker_ref, kv_ref, hidden_ref, gain_rows_ref, route_ref, weight_any, connector_any,
     hidden_grad_ref, own_sum_ref, swapped_ref, weight_sums_ref,
     talkers, kvs, hiddens, weight, connector,
-    local_rows, local_back, local_grad, packed, blocks, shifts, pick, rows, kv_rows, back, columns, terms, terms_in,
+    local_rows, local_grad, packed, blocks, shifts, pick, rows, kv_rows, back, columns, terms, terms_in,
     away, away_in, sums, sums_out, sums_in, total, gain_ref, send_sems, recv_sems, own_sems,
 ):
     bf16, f32 = jnp.bfloat16, jnp.float32
@@ -346,16 +346,13 @@
 
     def own_rows():
         mine = pl.ds(pl.multiple_of(place.t * share, share), share)
-        kv_all = kvs[...].reshape(slots, kvs.shape[2])
-        kv_rows[...] = dot(pick[...], kv_all, NN).astype(bf16)
 
         def first(i, carry):
             squares, products = carry
             tile = tile_of(i)
             inputs = dot(pick[mine, :], talkers[:, :, tile].reshape(slots, TILE), NN)
             local_rows[:, tile] = inputs
-            gained = gain_ref[:, tile] * dot(kv_rows[mine, :], weight[tile, :], NT)
-            local_back[:, tile] = gained
+            gained = back[mine, tile]
             return (
                 squares + jnp.sum(inputs * inputs, axis=1, keepdims=True),
                 products + jnp.sum(gained * inputs, axis=1, keepdims=True),
@@ -369,7 +366,7 @@
         def second(i, carry):
             tile = tile_of(i)
             scaled = local_rows[:, tile] * inv_rms
-            local_grad[:, tile] = (inv_rms * (local_back[:, tile] - scaled * mean)).astype(bf16)
+            local_grad[:, tile] = (inv_rms * (back[mine, tile] - scaled * mean)).astype(bf16)
             return carry
 
         lax.fori_loop(0, tiles, second, 0)
@@ -385,21 +382,37 @@
         for kind, offset in enumerate(offsets):
             shifts[kind] = onehot((window_at == wanted + offset) & (wanted < piece))
 
-    def pick_rows():
+    def pick_kv():
+        kv_all = kvs[...].reshape(slots, kvs.shape[2])
+        kv_rows[...] = dot(pick[...], kv_all, NN).astype(bf16)
         at = lax.broadcasted_iota(jnp.int32, columns_shape, 0)
         col = lax.broadcasted_iota(jnp.int32, columns_shape, 1)
         dp = ((at >> 2) & 1) * NZ + (at >> 3)
         chosen = onehot(col == (dp * n_tensor + place.t) * 4 + (at & 3))
         columns[...] = dot(chosen, kv_rows[...], NT).astype(bf16)
 
-        def one(i, squares):
+    def make_back(first, last):
+        def one(i, carry):
+            tile = tile_of(i)
+            back[:, tile] = gain_ref[:, tile] * dot(kv_rows[...], weight[tile, :], NT)
+            return carry
+
+        lax.fori_loop(first, last, one, 0)
+
+    def pick_rows():
+        def one(i, carry):
+            squares, products = carry
             tile = tile_of(i)
             inputs = dot(pick[...], talkers[:, :, tile].reshape(slots, TILE), NN)
             rows[:, tile] = inputs.astype(bf16)
-            return squares + jnp.sum(inputs * inputs, axis=1, keepdims=True)
-
-        squares = lax.fori_loop(0, tiles, one, jnp.zeros((rows_dev, 1), f32))
-        return lax.rsqrt(squares / width + 1e-06)
+            return (
+                squares + jnp.sum(inputs * inputs, axis=1, keepdims=True),
+                products + jnp.sum(back[:, tile] * inputs, axis=1, keepdims=True),
+            )
+
+        zero = jnp.zeros((rows_dev, 1), f32)
+        squares, products = lax.fori_loop(0, tiles, one, (zero, zero))
+        return lax.rsqrt(squares / width + 1e-06), products
 
     piece = width // (2 * NZ)
     starts = [min(i * piece // 128 * 128, width - WINDOW) for i in range(2 * NZ)]
@@ -417,15 +430,6 @@
             return carry
 
         lax.fori_loop(0, tiles, one, 0)
-
-    def make_back(first, last, products):
-        def one(i, products):
-            tile = tile_of(i)
-            gained = gain_ref[:, tile] * dot(kv_rows[...], weight[tile, :], NT)
-            back[:, tile] = gained
-            return products + jnp.sum(gained * rows[:, tile].astype(f32), axis=1, keepdims=True)
-
-        return lax.fori_loop(first, last, one, products)
 
     def make_hidden_grad(inv_rms, products):
         mean = products * inv_rms / width
@@ -474,21 +478,26 @@
     for direction in (0, 1):
         wide.take_far(0, direction)
         thin.take_far(0, direction)
-    for direction in (0, 1):
-        wide.take_y(1, direction, direction)
-    pass_z(2)
-    for direction in (0, 1):
-        wide.take_y(1, 1 - direction, direction)
-    for step in (0, 1, -1, 2):
+    for step in (0, 1, -1):
         for half in (0, 1):
             thin.take_x(step, half)
     for direction in (0, 1):
+        wide.take_y(1, direction, direction)
+    for half in (0, 1):
+        thin.take_x(2, half)
+    thin.take_shared()
+    kept[1].wait()
+    pick_kv()
+    loads[0].wait()
+    make_back(0, 3)
+    for direction in (0, 1):
+        wide.take_y(1, 1 - direction, direction)
+    pass_z(2)
+    make_back(3, tiles)
+    for direction in (0, 1):
         wide.take_far(1, direction)
-    thin.take_shared()
     wide.take_shared()
     kept[0].wait()
-    kept[1].wait()
-    loads[0].wait()
     own_rows()
     own_packed = pltpu.make_async_copy(
         packed.at[place.z], blocks.at[:, place.z, place.t], own_sems.at[5]
@@ -496,14 +505,13 @@
     own_packed.start()
     to_all_z(lambda step: packed.at[z_at(step)], blocks.at[:, place.z, place.t], packed_base)
     pass_z(3)
-    inv_rms = pick_rows()
+    inv_rms, products = pick_rows()
     make_terms(inv_rms)
     from_all_z(lambda step: blocks.at[:, z_at(step), place.t], packed_base)
     own_packed.wait()
     theirs.start((0,))
     ours.start((1,))
     to_all_z(lambda step: terms.at[z_at(step)], terms_in.at[place.z], terms_base)
-    products = make_back(0, tiles, jnp.zeros((rows_dev, 1), f32))
     ours.take_y(0, 1, 1)
     theirs.take_y(0, 0, 0)
     ours.take_y(0, 1, 0)
@@ -591,7 +599,6 @@
             pltpu.VMEM((NZ, rows_dev, d_dev), bf16),
             pltpu.VMEM(kv_weight.shape, bf16),
             pltpu.VMEM(connector.shape, bf16),
-            pltpu.VMEM((share, width), f32),
             pltpu.VMEM((share, width), f32),
             pltpu.VMEM((share, width), bf16),
             pltpu.VMEM((NZ, 2, share, BLOCK), bf16),

time: 72.5 us -> 76.5 us (1.055); the launches traced: 72.3 us -> 75.5 us
  Pallas kernels: 71.7 us -> 74.8 us
    pallas_call x1, Pallas kernels: 69.6 us -> 72.7 us  [on_device(): pl.pallas_call(whole, out_shape=(jax.ShapeDtypeStruct((rows_dev, d_dev),...]
where the time goes in v6:
time: 76.5 us; the launch traced here: 75.5 us
  Pallas kernels  74.8 us (98%)
    pallas_call x1, Pallas kernels, on_device(): pl.pallas_call(whole, out_shape=(jax.ShapeDtypeStruct((rows_dev, d_dev),...  72.7 us
    pallas_call x1, Pallas kernels, on_device(): pl.pallas_call(functools.partial(close, factor), out_shape=(jax.ShapeDtyp...  2.1 us

profile of v6, /device:TPU:1, one launch (start us, length us, event | category | flops | bytes accessed | tf_op | source)
XLA Modules:
  0.0 75.5 jit_solution(3550388015524366035)
XLA Ops:
  0.6 72.7 %shard_map.94 = (bf16[256,512]{1,0:T(8,128)(2,1)}, f32[224,512]{1,0:T(8,128)}, bf16[224,512]{1,0:T(8,128)(2,1)}, f32[8,3584]{1,0:T(8,128)}) custom-call(bf16[32,3584]{1,0:T(8,128)(2,1)} %talker_ref.1, bf16[32,1024]{1,0:T(8,128)(2,1)} %kv_ref.1, bf16[256,512]{1,0:T(8,128)(2,1)} %hidden_ref.1, f32[28,128]{1,0:T(8,128)} %bitcast.4, s32[1,256]{1,0:T(1,128)} %bitcast.5, ...), custom_call_target="tpu_custom_call" | custom-call | tf_op jit(solution)/shard_map/pallas_call | solution.py:586
  73.4 2.1 %shard_map.95 = (bf16[256,512]{1,0:T(8,128)(2,1)}, f32[224,512]{1,0:T(8,128)}, f32[4,3584]{1,0:T(4,128)}) custom-call(bf16[256,512]{1,0:T(8,128)(2,1)} %get-tuple-element.10.hidden_ref, f32[224,512]{1,0:T(8,128)} %get-tuple-element.11.own_ref, bf16[224,512]{1,0:T(8,128)(2,1)} %get-tuple-element.12.swapped_ref, f32[8,3584]{1,0:T(8,128)} %get-tuple-element.13.sums_ref), custom_call_target="tpu_custom_call" | custom-call | tf_op jit(solution)/shard_map/pallas_call | solution.py:638

commit v7 on v6

--- a/solution.py
+++ b/solution.py
@@ -478,24 +478,22 @@
     for direction in (0, 1):
         wide.take_far(0, direction)
         thin.take_far(0, direction)
-    for step in (0, 1, -1):
+    for direction in (0, 1):
+        wide.take_y(1, direction, direction)
+    pass_z(2)
+    for direction in (0, 1):
+        wide.take_y(1, 1 - direction, direction)
+    for step in (0, 1, -1, 2):
         for half in (0, 1):
             thin.take_x(step, half)
-    for direction in (0, 1):
-        wide.take_y(1, direction, direction)
-    for half in (0, 1):
-        thin.take_x(2, half)
     thin.take_shared()
     kept[1].wait()
     pick_kv()
     loads[0].wait()
     make_back(0, 3)
     for direction in (0, 1):
-        wide.take_y(1, 1 - direction, direction)
-    pass_z(2)
+        wide.take_far(1, direction)
     make_back(3, tiles)
-    for direction in (0, 1):
-        wide.take_far(1, direction)
     wide.take_shared()
     kept[0].wait()
     own_rows()

time: 76.5 us -> 73.4 us (0.959); the launches traced: 75.5 us -> 73.3 us
  Pallas kernels: 74.8 us -> 72.7 us
    pallas_call x1, Pallas kernels: 72.7 us -> 70.5 us  [on_device(): pl.pallas_call(whole, out_shape=(jax.ShapeDtypeStruct((rows_dev, d_dev),...]
where the time goes in v7:
time: 73.4 us; the launch traced here: 73.3 us
  Pallas kernels  72.7 us (99%)
    pallas_call x1, Pallas kernels, on_device(): pl.pallas_call(whole, out_shape=(jax.ShapeDtypeStruct((rows_dev, d_dev),...  70.5 us
    pallas_call x1, Pallas kernels, on_device(): pl.pallas_call(functools.partial(close, factor), out_shape=(jax.ShapeDtyp...  2.1 us

profile of v7, /device:TPU:1, one launch (start us, length us, event | category | flops | bytes accessed | tf_op | source)
XLA Modules:
  0.0 73.3 jit_solution(10619031062566955177)
XLA Ops:
  0.6 70.5 %shard_map.94 = (bf16[256,512]{1,0:T(8,128)(2,1)}, f32[224,512]{1,0:T(8,128)}, bf16[224,512]{1,0:T(8,128)(2,1)}, f32[8,3584]{1,0:T(8,128)}) custom-call(bf16[32,3584]{1,0:T(8,128)(2,1)} %talker_ref.1, bf16[32,1024]{1,0:T(8,128)(2,1)} %kv_ref.1, bf16[256,512]{1,0:T(8,128)(2,1)} %hidden_ref.1, f32[28,128]{1,0:T(8,128)} %bitcast.4, s32[1,256]{1,0:T(1,128)} %bitcast.5, ...), custom_call_target="tpu_custom_call" | custom-call | tf_op jit(solution)/shard_map/pallas_call | solution.py:584
  71.2 2.1 %shard_map.95 = (bf16[256,512]{1,0:T(8,128)(2,1)}, f32[224,512]{1,0:T(8,128)}, f32[4,3584]{1,0:T(4,128)}) custom-call(bf16[256,512]{1,0:T(8,128)(2,1)} %get-tuple-element.10.hidden_ref, f32[224,512]{1,0:T(8,128)} %get-tuple-element.11.own_ref, bf16[224,512]{1,0:T(8,128)(2,1)} %get-tuple-element.12.swapped_ref, f32[8,3584]{1,0:T(8,128)} %get-tuple-element.13.sums_ref), custom_call_target="tpu_custom_call" | custom-call | tf_op jit(solution)/shard_map/pallas_call | solution.py:636

commit v8 on v5

--- a/solution.py
+++ b/solution.py
@@ -476,9 +476,9 @@
         thin.take_far(0, direction)
     for direction in (0, 1):
         wide.take_y(1, direction, direction)
-    pass_z(2)
     for direction in (0, 1):
         wide.take_y(1, 1 - direction, direction)
+    pass_z(2)
     for step in (0, 1, -1, 2):
         for half in (0, 1):
             thin.take_x(step, half)

time: 72.5 us -> 72.5 us (level)
  no operation moved by 1% of the time
where the time goes in v8:
time: 72.5 us; the launch traced here: 72.3 us
  Pallas kernels  71.7 us (99%)
    pallas_call x1, Pallas kernels, on_device(): pl.pallas_call(whole, out_shape=(jax.ShapeDtypeStruct((rows_dev, d_dev),...  69.6 us
    pallas_call x1, Pallas kernels, on_device(): pl.pallas_call(functools.partial(close, factor), out_shape=(jax.ShapeDtyp...  2.1 us

profile of v8, /device:TPU:1, one launch (start us, length us, event | category | flops | bytes accessed | tf_op | source)
XLA Modules:
  0.0 72.3 jit_solution(4207806317456819653)
XLA Ops:
  0.6 69.6 %shard_map.94 = (bf16[256,512]{1,0:T(8,128)(2,1)}, f32[224,512]{1,0:T(8,128)}, bf16[224,512]{1,0:T(8,128)(2,1)}, f32[8,3584]{1,0:T(8,128)}) custom-call(bf16[32,3584]{1,0:T(8,128)(2,1)} %talker_ref.1, bf16[32,1024]{1,0:T(8,128)(2,1)} %kv_ref.1, bf16[256,512]{1,0:T(8,128)(2,1)} %hidden_ref.1, f32[28,128]{1,0:T(8,128)} %bitcast.4, s32[1,256]{1,0:T(1,128)} %bitcast.5, ...), custom_call_target="tpu_custom_call" | custom-call | tf_op jit(solution)/shard_map/pallas_call | solution.py:578
  70.2 2.1 %shard_map.95 = (bf16[256,512]{1,0:T(8,128)(2,1)}, f32[224,512]{1,0:T(8,128)}, f32[4,3584]{1,0:T(4,128)}) custom-call(bf16[256,512]{1,0:T(8,128)(2,1)} %get-tuple-element.10.hidden_ref, f32[224,512]{1,0:T(8,128)} %get-tuple-element.11.own_ref, bf16[224,512]{1,0:T(8,128)(2,1)} %get-tuple-element.12.swapped_ref, f32[8,3584]{1,0:T(8,128)} %get-tuple-element.13.sums_ref), custom_call_target="tpu_custom_call" | custom-call | tf_op jit(solution)/shard_map/pallas_call | solution.py:631
